TPU v7x, 128 devices: a whole 4x4x4 slice. The times are simulated.
128 devices in a mesh: cache: 32 (over x, y, z_lo), batch: 4 (over z_hi, core).
Axes of the slice: x: 4, y: 4, z: 4 (z_hi: 2, z_lo: 2; z = z_hi * 2 + z_lo), core: 2. Of those that a mesh axis runs over, the one named last changes fastest.
Arguments:
- queries: bfloat16 [3, 4096, 768], P(None, 'batch')
- positives: int32 [3, 4096], P(None, 'batch'), may hold values from 0 to 511
- block_list: int32 [3, 32, 192], P(None, 'batch'), may hold values from 0 to 255
- block_count: int32 [3, 32], P(None, 'batch'), may hold values from 1 to 192
- refresh_owner: int32 [3], replicated, may hold values from 0 to 31, as said below
- cache: float32 [32768, 768], P('cache'), may hold values from -6 to 6
- fresh: float32 [16384, 768], P('cache')
Outputs:
- query_grad: float32 [3, 4096, 768], P(None, ('batch', 'cache'))
- cache_grad: float32 [32768, 768], P('cache')
Inputs may be any that keep to these rules, and one draw needn't show every extreme that they name: `refresh_owner`: 3 different owners; owner 0 and owner 32 - 1 are always among them.
All inputs are finite; a program needn't handle non-finite values.
Results may differ from a plain program's by a relative error of at most 0.0003.
Values sent between devices are 32-bit elements; how exact they have to be, the bound alone decides.
A program may use at most 128 MiB of HBM per device.

v0:
```python
import math

import jax
import jax.numpy as jnp
from jax import lax
from jax.sharding import PartitionSpec as P

BLK = 128


def broadcast(block, axis, holder):
    block = jnp.where(lax.axis_index(axis) == holder, block, jnp.zeros_like(block))
    return lax.psum(block, axis)


def on_device(queries, positives, block_list, block_count, refresh_owner, cache, fresh):
    highest = lax.Precision.HIGHEST
    steps, group_rows, width = queries.shape
    cache_rows = cache.shape[0]
    slab_rows = fresh.shape[0]
    owners = lax.axis_size("cache")
    own_index = lax.axis_index("cache")
    share = group_rows // owners
    home_start = own_index * share
    group_blocks = block_list.shape[1]
    list_width = block_list.shape[2]
    own_blocks = cache_rows // BLK
    scale = 2.0 / math.sqrt(width)
    block_ids = own_index * own_blocks + jnp.arange(own_blocks, dtype=jnp.int32)
    current = cache
    grad_total = jnp.zeros((cache_rows, width), jnp.float32)
    results = []
    for step in range(steps):
        owner = refresh_owner[step]
        is_owner = owner == own_index
        refreshed = jnp.concatenate([fresh, current[slab_rows:]], axis=0)
        current = jnp.where(is_owner, refreshed, current)
        valid = jnp.arange(list_width, dtype=jnp.int32)[None, :] < block_count[step][:, None]
        hits = (block_list[step][:, :, None] == block_ids[None, None, :]) & valid[:, :, None]
        member = jnp.any(hits, axis=1)
        mask = jnp.broadcast_to(member[:, None, :, None], (group_blocks, BLK, own_blocks, BLK))
        mask = mask.reshape(group_rows, cache_rows)
        query_rows = queries[step].astype(jnp.float32)
        scores = scale * jnp.dot(query_rows, current.T, precision=highest)
        scores = jnp.where(mask, scores, -1e30)
        peak = jnp.max(scores, axis=1)
        slab = broadcast(fresh, "cache", owner)
        home_queries = lax.dynamic_slice_in_dim(query_rows, home_start, share, 0)
        slab_scores = scale * jnp.dot(home_queries, slab.T, precision=highest)
        filler = jnp.full((group_rows,), -1e30, jnp.float32)
        slab_peak = lax.dynamic_update_slice_in_dim(
            filler, jnp.max(slab_scores, axis=1), home_start, 0
        )
        peak = jnp.maximum(peak, slab_peak)
        top = lax.pmax(peak, "cache")
        total = jnp.sum(jnp.where(mask, jnp.exp(scores - top[:, None]), 0.0), axis=1)
        home_top = lax.dynamic_slice_in_dim(top, home_start, share, 0)
        slab_total = jnp.sum(jnp.exp(slab_scores - home_top[:, None]), axis=1)
        home_part = lax.dynamic_slice_in_dim(total, home_start, share, 0) + slab_total
        total = lax.dynamic_update_slice_in_dim(total, home_part, home_start, 0)
        total = lax.psum(total, "cache")
        lse = top + jnp.log(total)
        probs = jnp.exp(scores - lse[:, None])
        home_lse = lax.dynamic_slice_in_dim(lse, home_start, share, 0)
        slab_probs = jnp.exp(slab_scores - home_lse[:, None])
        home_pos = lax.dynamic_slice_in_dim(positives[step], home_start, share, 0)
        home_term = jnp.dot(slab_probs, slab, precision=highest) - jnp.take(slab, home_pos, axis=0)
        term = jnp.dot(probs, current, precision=highest)
        mine = lax.psum_scatter(term, "cache", scatter_dimension=0, tiled=True)
        mine = mine + home_term
        results.append(mine)
        step_grad = lax.dot_general(probs, query_rows, (((0,), (0,)), ((), ())), precision=highest)
        grad_total = grad_total + lax.psum(step_grad, "batch")
    return (jnp.stack(results, axis=0), grad_total)


def solution(mesh):
    return jax.shard_map(
        on_device,
        mesh=mesh,
        in_specs=(
            P(None, "batch", None),
            P(None, "batch"),
            P(None, "batch", None),
            P(None, "batch"),
            P(),
            P("cache", None),
            P("cache", None),
        ),
        out_specs=(P(None, ("batch", "cache"), None), P("cache", None)),
        check_vma=False,
    )
```

profile of v0, /device:TPU:0, one launch (start us, length us, event | category | flops | bytes accessed | tf_op | source)
XLA Modules:
  0.0 1260.2 jit_solution(4495534913368518108)
XLA Ops:
  10.5 3.7 broadcast_select_fusion.2
  23.8 4.9 fusion.60
  29.1 9.3 fusion.65
  38.7 7.3 fusion.67
  47.3 7.4 fusion.63
  54.8 288.5 %all-reduce.8.cloned.1.call-done = (f32[512,768]{1,0:T(8,128)}, f32[512,768]{1,0:T(8,128)}, f32[512,768]{1,0:T(8,128)}) async-done(((f32[512,768]{1,0:T(8,128)}, f32[512,768]{1,0:T(8,128)}, f32[512,768]{1,0:T(8,128)}), (f32[512,768]{1,0:T(8,128)}, f32[512,768]{1,0:T(8,128)}, f32[512,768]{1,0:T(8,128)})) %all-reduce.8.cloned.1.call-update) | async-done | bytes 4718608 | tf_op jit(solution)/shard_map/psum | solution.py:13
  343.2 2.5 fusion.64
  351.1 157.2 %all-reduce.2 = (f32[1024]{0:T(1024)S(1)}, f32[1024]{0:T(1024)S(1)}, f32[1024]{0:T(1024)S(1)}) all-reduce(f32[1024]{0:T(1024)S(1)} %max.17, f32[1024]{0:T(1024)S(1)} %max.16, f32[1024]{0:T(1024)S(1)} %max.15), channel_id=1, replica_groups=mesh['cache'=32,'batch'=4] {'cache'}, use_global_device_ids=true, to_apply=%region_22.24 | all-reduce | flops 3072 | bytes 24576 | tf_op jit(solution)/shard_map/pmax | solution.py:55
  508.5 3.7 select_reduce_fusion
  516.8 152.1 %all-reduce = (f32[1024]{0:T(1024)S(1)}, f32[1024]{0:T(1024)S(1)}, f32[1024]{0:T(1024)S(1)}) all-reduce(f32[1024]{0:T(1024)S(1)} %add_dynamic-update-slice_fusion, f32[1024]{0:T(1024)S(1)} %add_dynamic-update-slice_fusion.1, f32[1024]{0:T(1024)S(1)} %add_dynamic-update-slice_fusion.2), channel_id=1, replica_groups=mesh['cache'=32,'batch'=4] {'cache'}, use_global_device_ids=true, to_apply=%region_25.27 | all-reduce | flops 3072 | bytes 24576 | tf_op jit(solution)/shard_map/psum | solution.py:61
  668.9 14.5 %fusion.5 = f32[1024,768]{1,0:T(8,128)} fusion(f32[1024,1024]{0,1:T(8,128)} %get-tuple-element.40, f32[1024]{0:T(1024)S(1)} %log_add_fusion, f32[1024,768]{1,0:T(8,128)} %copy-done.4, f32[512,768]{1,0:T(8,128)S(1)} %copy-done, f32[512,768]{1,0:T(8,128)S(1)} %copy-done.13, pred[]{:T(512)S(6)} %eq.73), kind=kOutput, calls=%fused_computation.20 | convolution fusion | flops 9666297856 | bytes 13635585 | tf_op jit(solution)/shard_map/dot_general | solution.py:68
  685.3 13.5 %fusion.3 = f32[1024,768]{1,0:T(8,128)} fusion(f32[1024,768]{1,0:T(8,128)S(1)} %copy-done.6, f32[1024,1024]{0,1:T(8,128)} %get-tuple-element.44, f32[1024]{0:T(1024)S(1)} %log_add_fusion.1), kind=kOutput, calls=%fused_computation.18 | convolution fusion | flops 9664724992 | bytes 10489856 | tf_op jit(solution)/shard_map/dot_general | solution.py:68
  700.8 13.4 %fusion.1 = f32[1024,768]{1,0:T(8,128)} fusion(f32[1024,768]{1,0:T(8,128)S(1)} %copy-done.3, f32[1024,1024]{0,1:T(8,128)} %get-tuple-element.48, f32[1024]{0:T(1024)S(1)} %log_add_fusion.2), kind=kOutput, calls=%fused_computation.16 | convolution fusion | flops 9664724992 | bytes 10489856 | tf_op jit(solution)/shard_map/dot_general | solution.py:68
  714.3 8.2 fusion
  722.5 7.2 fusion.2
  729.8 8.8 add_add_fusion
  740.2 2.7 gather_fusion.2
  744.8 101.3 %reduce-scatter.8.cloned.1.call-done = f32[32,768]{1,0:T(8,128)} async-done(((f32[1024,768]{1,0:T(8,128)}), f32[32,768]{1,0:T(8,128)}) %reduce-scatter.8.cloned.1.call-update) | async-done | bytes 98320 | tf_op jit(solution)/shard_map/reduce_scatter | solution.py:69
  846.1 2.7 fusion.24
  848.8 161.9 %reduce-scatter.6.cloned.1.call-done = f32[32,768]{1,0:T(8,128)} async-done(((f32[1024,768]{1,0:T(8,128)}), f32[32,768]{1,0:T(8,128)}) %reduce-scatter.6.cloned.1.call-update) | async-done | bytes 98320 | tf_op jit(solution)/shard_map/reduce_scatter | solution.py:69
  1010.7 2.6 fusion.26
  1013.3 161.4 %reduce-scatter.4.cloned.1.call-done = f32[32,768]{1,0:T(8,128)} async-done(((f32[1024,768]{1,0:T(8,128)}), f32[32,768]{1,0:T(8,128)}) %reduce-scatter.4.cloned.1.call-update) | async-done | bytes 98320 | tf_op jit(solution)/shard_map/reduce_scatter | solution.py:69
  1178.2 71.4 %all-reduce.6.cloned.1.call-done = f32[1024,768]{1,0:T(8,128)} async-done(((f32[1024,768]{1,0:T(8,128)}), f32[1024,768]{1,0:T(8,128)}) %all-reduce.6.cloned.1.call-update) | async-done | bytes 3145744 | tf_op jit(solution)/shard_map/psum | solution.py:73
  1249.6 3.8 copy.31
  (123 shorter events, 31.6 us)
Async XLA Ops:
  7.2 336.1 %all-reduce.8.cloned.1.call-start = ((), (), s32[]{:S(2)}) async-start(), calls=%async_computation.7 | async-start | bytes 9437184 | tf_op jit(solution)/shard_map/psum | solution.py:13
  14.2 2.3 copy-start
  14.2 2.3 slice-start
  14.3 831.9 %reduce-scatter.8.cloned.1.call-start = ((), (), s32[]{:S(2)}) async-start(), calls=%async_computation.5 | async-start | bytes 3244032 | tf_op jit(solution)/shard_map/reduce_scatter | solution.py:69
  22.2 24.1 %copy-start.12 = (f32[512,768]{1,0:T(8,128)}, f32[512,768]{1,0:T(8,128)S(1)}, u32[]{:S(2)}) copy-start(f32[512,768]{1,0:T(8,128)S(1)} %slice.79) | copy-start | bytes 4718596
  23.8 5.2 copy-start.5
  28.7 10.0 slice-start.1
  29.0 9.3 copy-start.17
  29.0 9.7 copy-start.2
  29.0 9.7 slice-start.2
  38.7 7.3 copy-start.19
  343.2 5.5 copy-start.8
  350.5 161.8 %copy-start.18 = (pred[8,128,8,128]{1,0,3,2:T(8,128)(4,1)S(1)}, pred[8,128,8,128]{1,0,3,2:T(8,128)(4,1)}, u32[]{:S(2)}) copy-start(pred[8,128,8,128]{1,0,3,2:T(8,128)(4,1)} %copy-done.17) | copy-start | bytes 3145732
  508.4 3.9 copy-start.14
  512.2 2.5 copy-start.20
  513.4 155.5 %copy-start.13 = (f32[512,768]{1,0:T(8,128)S(1)}, f32[512,768]{1,0:T(8,128)}, u32[]{:S(2)}) copy-start(f32[512,768]{1,0:T(8,128)} %copy-done.12) | copy-start | bytes 4718596
  683.4 327.2 %reduce-scatter.6.cloned.1.call-start = ((), (), s32[]{:S(2)}) async-start(), calls=%async_computation.4 | async-start | bytes 3244032 | tf_op jit(solution)/shard_map/reduce_scatter | solution.py:69
  698.9 475.8 %reduce-scatter.4.cloned.1.call-start = ((), (), s32[]{:S(2)}) async-start(), calls=%async_computation.3 | async-start | bytes 3244032 | tf_op jit(solution)/shard_map/reduce_scatter | solution.py:69
  714.2 535.4 %all-reduce.6.cloned.1.call-start = ((), (), s32[]{:S(2)}) async-start(), calls=%async_computation.6 | async-start | bytes 6291456 | tf_op jit(solution)/shard_map/psum | solution.py:73
  714.2 8.2 copy-start.15
  722.5 7.3 copy-start.7
  729.8 8.8 copy-start.23
  738.5 4.4 copy-start.10
  738.6 5.6 copy-start.9
  (9 other events, 13.7 us)
Sparse Core Ops, SparseCore 0:
  14.4 328.7 all-reduce.7
  683.6 162.5 reduce-scatter.7
  849.2 161.4 reduce-scatter.5
  1012.9 161.6 reduce-scatter.3
  1177.2 72.3 all-reduce.5
where the time goes:
time: 1260 us
  waiting for transfers between devices  785 us (62%)
  blocking collectives  309 us (25%)
  matrix products  104 us (8%)
  local copies, waits for them, and re-layouts  29.8 us (2%)
  between operations  18.6 us (1%)
  other arithmetic  14.1 us (1%)
    reduce_scatter x3, waiting for transfers between devices, on_device(): mine = lax.psum_scatter(term, 'cache', scatter_dimension=0, tiled=True)  425 us
    psum x1, waiting for transfers between devices, broadcast(): return lax.psum(block, axis)  288 us
    pmax x1, blocking collectives, on_device(): top = lax.pmax(peak, 'cache')  157 us
    psum x1, blocking collectives, on_device(): total = lax.psum(total, 'cache')  152 us
    psum x1, waiting for transfers between devices, on_device(): grad_total = grad_total + lax.psum(step_grad, 'batch')  71.4 us
    dot_general x3, matrix products, on_device(): term = jnp.dot(probs, current, precision=highest)  41.5 us
  transfers between devices with their start and end apart: 5, of which 5 were waited for; matrix products, arithmetic and copies ran while one was open for 8% of the time, Pallas kernels for 0%

commit v1 on v0

v1 whole, which is shorter than its diff:
```python
import functools
import math

import jax
import jax.numpy as jnp
from jax import lax
from jax.experimental import pallas as pl
from jax.experimental.pallas import tpu as pltpu
from jax.sharding import PartitionSpec as P

BLK = 128
RING = 4
NEG = -1e30
F32 = jnp.float32
BF16 = jnp.bfloat16
NT = (((1,), (1,)), ((), ()))
TN = (((0,), (0,)), ((), ()))
NN = (((1,), (0,)), ((), ()))
ORDER = (2, 1, 3, 0)


def mm(a, b, dims):
    return lax.dot_general(a, b, dims, preferred_element_type=F32)


def halves(x):
    high = x.astype(BF16)
    return high, (x - high.astype(F32)).astype(BF16)


def kernel(
    q_hbm, pos_ref, list_ref, count_ref, owner_ref, cache_hbm, fresh_hbm,
    qg_hbm, cg_hbm,
    q, chi, clo, e, zs, ah, al, mloc, keep, factor, factor_w, posx, lse,
    stat_out, stat_in, t, r1, u, r2, r3, g, pair_in, far_in,
    in_sem, out_sem, send_sem, recv_sem,
):
    steps = q.shape[0]
    rows = q.shape[1] // RING
    width = q.shape[2]
    cols = chi.shape[1]
    blocks = cols // BLK
    slab = fresh_hbm.shape[0]
    slab_blocks = slab // BLK
    quarter = rows // RING
    part = quarter // 2
    half = rows // 2
    list_width = list_ref.shape[2]
    scale = 2.0 / math.sqrt(width)
    log2e = math.log2(math.e)

    ci = lax.axis_index("cache")
    bi = lax.axis_index("batch")
    x, y, zl = ci // 8, (ci // 2) % 4, ci % 2
    zh, core = bi // 2, bi % 2
    one, two = 1 - core, core
    own_a = x * one + y * two
    own_b = y * one + x * two

    def first(d):
        return (((x + d * one) % 4) * 8 + ((y + d * two) % 4) * 2 + zl, bi)

    def second(d):
        return (((x + d * two) % 4) * 8 + ((y + d * one) % 4) * 2 + zl, bi)

    z_peer = (ci + 1 - 2 * zl, bi)
    far_peer = (ci, (1 - zh) * 2 + core)
    pair_peer = (ci, zh * 2 + 1 - core)
    peers = [first(1), first(2), first(3), second(1), second(2), second(3), z_peer, far_peer, pair_peer]

    def remote(number, src, dst, device):
        return pltpu.make_async_remote_copy(
            src_ref=src, dst_ref=dst, send_sem=send_sem.at[number], recv_sem=recv_sem.at[number],
            device_id=device, device_id_type=pl.DeviceIdType.MESH,
        )

    barrier = pltpu.get_barrier_semaphore()
    for peer in peers:
        pl.semaphore_signal(barrier, inc=1, device_id=peer, device_id_type=pl.DeviceIdType.MESH)

    load_c = pltpu.make_async_copy(cache_hbm, g, in_sem.at[0])
    load_c.start()
    loads_f = []
    for i in range(slab // rows):
        loads_f.append(pltpu.make_async_copy(fresh_hbm.at[pl.ds(i * rows, rows)], u.at[i], in_sem.at[1 + i]))
        loads_f[-1].start()
    q_sem = 1 + slab // rows
    for s in range(steps):
        @pl.loop(0, RING * RING)
        def _(i, s=s):
            a, b = i // RING, i % RING
            src = (a * one + b * two) * rows + (b * one + a * two) * quarter
            pltpu.make_async_copy(
                q_hbm.at[s, pl.ds(pl.multiple_of(src, quarter), quarter)],
                q.at[s, pl.ds(pl.multiple_of(i * quarter, quarter), quarter)],
                in_sem.at[q_sem + s],
            ).start()

    lanes = lax.broadcasted_iota(jnp.int32, (blocks, rows), 1)
    slot = lax.broadcasted_iota(jnp.int32, (1, list_width), 1)
    ids = ci * blocks + lax.broadcasted_iota(jnp.int32, (blocks, 1), 0)
    low_lanes = lax.broadcasted_iota(jnp.int32, (8, BLK), 1) < quarter

    def tables(s):
        @pl.loop(0, RING)
        def _(a):
            c = s * RING + a
            listed = jnp.zeros((blocks, rows), F32)
            picked = []
            for b in range(RING):
                block = (2 * a + b // 2) * one + (2 * b + a // 2) * two
                row = list_ref[s, pl.ds(block, 1), :]
                valid = slot < count_ref[s, block]
                hit = jnp.where((row == ids) & valid, 1.0, 0.0)
                hit = jnp.max(hit, axis=1, keepdims=True)
                listed = jnp.where(lanes // quarter == b, hit, listed)
                tile = (2 * a + b // 2) * one + (2 * b + a // 2) * two
                found = pos_ref[pl.ds(s, 1), pl.ds(pl.multiple_of(tile * BLK, BLK), BLK)]
                found = jnp.broadcast_to(found, (8, BLK))
                side = (b % 2) * one + (a % 2) * two
                flag = jnp.broadcast_to(side, (8, BLK)) == b % 2
                picked.append(jnp.where(flag, found, pltpu.roll(found, quarter, 1)))
            keep[c] = listed
            mine = jnp.broadcast_to(owner_ref[s], (8, BLK)) == ci
            for i in range(2):
                both = jnp.where(low_lanes, picked[2 * i], picked[2 * i + 1])
                posx[c, :, i * BLK:(i + 1) * BLK] = jnp.where(mine, both, -1)

    def weights(s, c):
        mine = jnp.broadcast_to(owner_ref[s], (blocks, rows)) == ci
        top = lax.broadcasted_iota(jnp.int32, (blocks, rows), 0) < slab_blocks
        return keep[c] + jnp.where(mine & top, 1.0, 0.0)

    def prepare():
        @pl.loop(0, cols // BLK)
        def _(i):
            at = pl.ds(pl.multiple_of(i * BLK, BLK), BLK)
            high, low = halves(g[at, :])
            for s in range(steps):
                chi[s, at, :] = high
                clo[s, at, :] = low

        @pl.loop(0, slab // BLK)
        def _(i):
            at = pl.ds(pl.multiple_of(i * BLK, BLK), BLK)
            per = rows // BLK
            old = g[at, :]
            new = u[i // per, pl.ds(pl.multiple_of((i % per) * BLK, BLK), BLK), :]
            done = jnp.zeros((BLK, width), jnp.bool_)
            for s in range(steps):
                done = done | (jnp.broadcast_to(owner_ref[s], (BLK, width)) == ci)
                high, low = halves(jnp.where(done, new, old))
                chi[s, at, :] = high
                clo[s, at, :] = low

    def scores(s, begin, count):
        @pl.loop(begin, begin + count)
        def _(a):
            c = s * RING + a
            block_q = q[s, pl.ds(pl.multiple_of(a * rows, rows), rows), :]
            zs[...] = mm(chi[s], block_q, NT) + mm(clo[s], block_q, NT)
            sums = []
            for j in range(blocks):
                at = slice(j * BLK, (j + 1) * BLK)
                z = zs[at, :]
                peak = jnp.max(z, axis=0, keepdims=True)
                value = jnp.exp2((z - peak) * (scale * log2e))
                e[c, at, :] = value
                mloc[c, j:j + 1, :] = peak * scale
                sums.append(jnp.sum(value, axis=0, keepdims=True))
            w = weights(s, c)
            peaks = jnp.where(w > 0.0, mloc[c], NEG)
            top = jnp.max(peaks, axis=0, keepdims=True)
            total = jnp.concatenate(sums, axis=0) * jnp.exp(peaks - top)
            total = jnp.sum(jnp.where(w > 0.0, w * total, 0.0), axis=0, keepdims=True)
            stat_out[s, 0, pl.ds(a, 1), :] = top
            stat_out[s, 0, pl.ds(RING + a, 1), :] = total

    def stat_copy(s, stage):
        base = s * 7 + stage * 3
        if stage == 2:
            return [remote(base, stat_out.at[s, 2], stat_in.at[s, 2, 0], z_peer)]
        where = first if stage == 0 else second
        return [remote(base + d - 1, stat_out.at[s, stage], stat_in.at[s, stage, d - 1], where(d)) for d in (1, 2, 3)]

    sent = []

    def stat_send(s, stage):
        for copy in stat_copy(s, stage):
            copy.start()
            sent.append(copy)

    def stat_merge(s, stage):
        copies = stat_copy(s, stage)
        for copy in copies:
            copy.wait_recv()
        got = [stat_out[s, stage]] + [stat_in[s, stage, i] for i in range(len(copies))]
        tops = [v[:RING] for v in got]
        top = functools.reduce(jnp.maximum, tops)
        total = sum(v[RING:] * jnp.exp(p - top) for v, p in zip(got, tops))
        if stage < 2:
            stat_out[s, stage + 1, :RING, :] = top
            stat_out[s, stage + 1, RING:, :] = total
            stat_send(s, stage + 1)
            return
        lse[s, :RING, :] = top + jnp.log(total)
        for a in range(RING):
            c = s * RING + a
            scaled = jnp.exp(mloc[c] - lse[s, a:a + 1, :])
            w = weights(s, c)
            factor[c] = jnp.where(keep[c] > 0.0, scaled, 0.0)
            factor_w[c] = jnp.where(w > 0.0, w * scaled, 0.0)

    def ring1(s, i):
        right, left = first(1), first(3)
        low, high = pl.ds(0, half), pl.ds(half, half)
        src, device = [
            (t.at[s, 0, low], right), (t.at[s, 0, high], left),
            (t.at[s, 1, high], right), (t.at[s, 1, low], right),
            (t.at[s, 2, low], left), (t.at[s, 2, high], left),
        ][i]
        return remote(21 + s * 13 + i, src, r1.at[s, i], device)

    def start(copy):
        copy.start()
        sent.append(copy)

    def terms(s):
        @pl.loop(0, RING)
        def _(k):
            hop = jnp.where(k == 0, 2, jnp.where(k == 1, 1, jnp.where(k == 2, 3, 0)))
            a = (own_a + hop) % RING
            c = s * RING + a
            place = posx[c, 0:1, :]
            for j in range(blocks):
                at = slice(j * BLK, (j + 1) * BLK)
                value = e[c, at, :] * factor_w[c, j:j + 1, :]
                if j < slab_blocks:
                    row = lax.broadcasted_iota(jnp.int32, (BLK, rows), 0) + j * BLK
                    value = value - jnp.where(row == place, 1.0, 0.0)
                ah[at, :], al[at, :] = halves(value)
            t[s, k] = mm(ah[...], chi[s], TN) + mm(ah[...], clo[s], TN) + mm(al[...], chi[s], TN)

            @pl.when(k == 0)
            def _():
                ring1(s, 0).start()
                ring1(s, 1).start()

            @pl.when(k == 1)
            def _():
                ring1(s, 2).start()

            @pl.when(k == 2)
            def _():
                ring1(s, 4).start()

        sent.extend(ring1(s, i) for i in (0, 1, 2, 4))

    def relay1(s):
        ring1(s, 0).wait_recv()
        t[s, 1, :half, :] += r1[s, 0]
        start(ring1(s, 3))
        ring1(s, 1).wait_recv()
        t[s, 2, half:, :] += r1[s, 1]
        start(ring1(s, 5))

    def piece(s, d, side):
        at = ((own_b + d) % RING) * quarter + side * part
        return u.at[s, pl.ds(pl.multiple_of(at, part), part)]

    def ring2(s, i):
        right, left = second(1), second(3)
        d, side, device = [(2, 0, right), (2, 1, left), (1, 1, right), (1, 0, right), (3, 0, left), (3, 1, left)][i]
        return remote(21 + s * 13 + 6 + i, piece(s, d, side), r2.at[s, i], device)

    def finish1(s):
        for i in (2, 3, 4, 5):
            ring1(s, i).wait_recv()
        u[s, :half, :] = t[s, 3, :half, :] + r1[s, 3] + r1[s, 4]
        u[s, half:, :] = t[s, 3, half:, :] + r1[s, 2] + r1[s, 5]
        for i in (0, 1, 2, 4):
            start(ring2(s, i))

    def relay2(s):
        ring2(s, 0).wait_recv()
        ref = piece(s, 1, 0)
        ref[...] += r2[s, 0]
        start(ring2(s, 3))
        ring2(s, 1).wait_recv()
        ref = piece(s, 3, 1)
        ref[...] += r2[s, 1]
        start(ring2(s, 5))

    def last(s):
        return remote(21 + s * 13 + 12, piece(s, 0, 1 - zl), r3.at[s], z_peer)

    def finish2(s):
        for i in (2, 3, 4, 5):
            ring2(s, i).wait_recv()
        ref = piece(s, 0, 0)
        ref[...] += r2[s, 3] + r2[s, 4]
        ref = piece(s, 0, 1)
        ref[...] += r2[s, 2] + r2[s, 5]
        start(last(s))

    def finish3(s):
        last(s).wait_recv()
        ref = piece(s, 0, zl)
        ref[...] += r3[s]
        out_copy(s).start()

    def out_copy(s):
        return pltpu.make_async_copy(piece(s, 0, zl), qg_hbm.at[s], out_sem.at[s])

    side_rows = cols // 2
    other_at = pl.ds(pl.multiple_of((1 - core) * side_rows, side_rows), side_rows)
    mine_at = pl.ds(pl.multiple_of(core * side_rows, side_rows), side_rows)
    base = 21 + steps * 13
    pair_copy = remote(base, g.at[other_at], pair_in, pair_peer)
    far_copy = remote(base + 1, g.at[mine_at], far_in, far_peer)
    final_copy = remote(base + 2, g.at[mine_at], cg_hbm.at[mine_at], pair_peer)
    final_local = pltpu.make_async_copy(g.at[mine_at], cg_hbm.at[mine_at], out_sem.at[steps])

    def gradient(side, at):
        g[at, :] = jnp.zeros((side_rows, width), F32)

        @pl.loop(0, steps * RING)
        def _(c):
            s, a = c // RING, c % RING
            for j in range(side_rows // BLK):
                where = pl.ds(pl.multiple_of(side * side_rows, side_rows) + j * BLK, BLK)
                scaled = factor[c, pl.ds(side * (side_rows // BLK) + j, 1), :]
                put = slice(j * BLK, (j + 1) * BLK)
                ah[put, :], al[put, :] = halves(e[c, where, :] * scaled)
            block_q = q[s, pl.ds(pl.multiple_of(a * rows, rows), rows), :]
            g[at, :] += mm(ah[:side_rows, :], block_q, NN) + mm(al[:side_rows, :], block_q, NN)

    load_c.wait()
    for load in loads_f:
        load.wait()
    prepare()
    for s in range(steps):
        tables(s)

    def q_ready(s):
        pltpu.make_async_copy(q_hbm.at[s], q.at[s], in_sem.at[q_sem + s]).wait()

    q_ready(0)
    scores(0, 0, RING)
    pl.semaphore_wait(barrier, len(peers))
    stat_send(0, 0)
    q_ready(1)
    scores(1, 0, 2)
    stat_merge(0, 0)
    scores(1, 2, 2)
    stat_merge(0, 1)
    stat_send(1, 0)
    q_ready(2)
    scores(2, 0, 1)
    stat_merge(0, 2)
    terms(0)
    stat_merge(1, 0)
    scores(2, 1, 1)
    stat_merge(1, 1)
    relay1(0)
    scores(2, 2, 2)
    stat_send(2, 0)
    stat_merge(1, 2)
    terms(1)
    stat_merge(2, 0)
    finish1(0)
    relay1(1)
    stat_merge(2, 1)
    relay2(0)
    stat_merge(2, 2)
    gradient(1 - core, other_at)
    pair_copy.start()
    terms(2)
    finish2(0)
    finish1(1)
    relay1(2)
    finish3(0)
    relay2(1)
    gradient(core, mine_at)
    pair_copy.wait_recv()
    g[mine_at, :] += pair_in[...]
    far_copy.start()
    finish2(1)
    finish1(2)
    finish3(1)
    relay2(2)
    finish2(2)
    finish3(2)
    far_copy.wait()
    g[mine_at, :] += far_in[...]
    final_copy.start()
    final_local.start()
    for copy in sent:
        copy.wait_send()
    pair_copy.wait_send()
    for s in range(steps):
        out_copy(s).wait()
    final_local.wait()
    final_copy.wait()


def on_device(queries, positives, block_list, block_count, refresh_owner, cache, fresh):
    steps, group_rows, width = queries.shape
    cols = cache.shape[0]
    owners = lax.axis_size("cache")
    share = group_rows // owners
    rows = group_rows // RING
    chunks = steps * RING
    blocks = cols // BLK
    half, part = rows // 2, rows // RING // 2
    messages = 21 + steps * 13 + 3
    vmem = pl.BlockSpec(memory_space=pltpu.VMEM)
    smem = pl.BlockSpec(memory_space=pltpu.SMEM)
    anywhere = pl.BlockSpec(memory_space=pl.ANY)
    small = pltpu.VMEM((chunks, blocks, rows), F32)
    return pl.pallas_call(
        kernel,
        out_shape=(
            jax.ShapeDtypeStruct((steps, share, width), F32),
            jax.ShapeDtypeStruct((cols, width), F32),
        ),
        in_specs=[anywhere, vmem, vmem, smem, smem, anywhere, anywhere],
        out_specs=(anywhere, anywhere),
        scratch_shapes=[
            pltpu.VMEM((steps, group_rows, width), BF16),
            pltpu.VMEM((steps, cols, width), BF16),
            pltpu.VMEM((steps, cols, width), BF16),
            pltpu.VMEM((chunks, cols, rows), F32),
            pltpu.VMEM((cols, rows), F32),
            pltpu.VMEM((cols, rows), BF16),
            pltpu.VMEM((cols, rows), BF16),
            small, small, small, small,
            pltpu.VMEM((chunks, 8, rows), jnp.int32),
            pltpu.VMEM((steps, 8, rows), F32),
            pltpu.VMEM((steps, 3, 8, rows), F32),
            pltpu.VMEM((steps, 3, 3, 8, rows), F32),
            pltpu.VMEM((steps, RING, rows, width), F32),
            pltpu.VMEM((steps, 6, half, width), F32),
            pltpu.VMEM((steps, rows, width), F32),
            pltpu.VMEM((steps, 6, part, width), F32),
            pltpu.VMEM((steps, part, width), F32),
            pltpu.VMEM((cols, width), F32),
            pltpu.VMEM((cols // 2, width), F32),
            pltpu.VMEM((cols // 2, width), F32),
            pltpu.SemaphoreType.DMA((1 + fresh.shape[0] // rows + steps,)),
            pltpu.SemaphoreType.DMA((steps + 1,)),
            pltpu.SemaphoreType.DMA((messages,)),
            pltpu.SemaphoreType.DMA((messages,)),
        ],
        compiler_params=pltpu.CompilerParams(
            collective_id=0, has_side_effects=True, vmem_limit_bytes=67_043_328
        ),
        name="cache_step",
    )(queries, positives, block_list, block_count, refresh_owner, cache, fresh)


def solution(mesh):
    return jax.shard_map(
        on_device,
        mesh=mesh,
        in_specs=(
            P(None, "batch", None),
            P(None, "batch"),
            P(None, "batch", None),
            P(None, "batch"),
            P(),
            P("cache", None),
            P("cache", None),
        ),
        out_specs=(P(None, ("batch", "cache"), None), P("cache", None)),
        check_vma=False,
    )
```

time: 1260 us -> 127 us (0.10)
  waiting for transfers between devices: 785 us -> 0 us
  blocking collectives: 309 us -> 0 us
  Pallas kernels: 0 us -> 120 us
  matrix products: 104 us -> 0 us
  local copies, waits for them, and re-layouts: 29.8 us -> 5.45 us
  between operations: 18.6 us -> 0.64 us
  other arithmetic: 14.1 us -> 0 us
    reduce_scatter x3 -> x0, waiting for transfers between devices: 425 us -> none  [on_device(): mine = lax.psum_scatter(term, 'cache', scatter_dimension=0, tiled=True)]
    psum x2 -> x0, waiting for transfers between devices: 360 us -> none  [the longest x1 288 us: broadcast(): return lax.psum(block, axis)]
    pmax x1 -> x0, blocking collectives: 157 us -> none  [on_device(): top = lax.pmax(peak, 'cache')]
    psum x1 -> x0, blocking collectives: 152 us -> none  [on_device(): total = lax.psum(total, 'cache')]
    pallas_call x0 -> x1, Pallas kernels: none -> 120 us  [on_device(): pl.pallas_call(kernel, out_shape=(jax.ShapeDtypeStruct((steps, share, wid...]
    dot_general x15 -> x0, matrix products: 104 us -> none  [the longest x3 41.5 us: on_device(): term = jnp.dot(probs, current, precision=highest)]
  transfers between devices with their start and end apart: 5 -> 0, of which waited for: 5 -> 0; matrix products, arithmetic and copies ran while one was open for 8% -> 0% of each run, Pallas kernels for 0% -> 0%
where the time goes in v1:
time: 127 us; the launch traced here: 126 us
  Pallas kernels  120 us (94%)
  local copies, waits for them, and re-layouts  5.45 us (4%)
    pallas_call x1, Pallas kernels, on_device(): pl.pallas_call(kernel, out_shape=(jax.ShapeDtypeStruct((steps, share, wid...  120 us
    unnamed x2, local copies, waits for them, and re-layouts  5.45 us

profile of v1, /device:TPU:0, one launch (start us, length us, event | category | flops | bytes accessed | tf_op | source)
XLA Modules:
  0.0 125.9 jit_solution(10184403699968957864)
XLA Ops:
  0.6 119.8 %cache_step.1 = (f32[3,32,768]{2,1,0:T(8,128)}, f32[1024,768]{1,0:T(8,128)}) custom-call(bf16[3,1024,768]{2,1,0:T(8,128)(2,1)} %q_hbm.1, s32[3,1024]{1,0:T(4,128)} %pos_ref.1, s32[3,8,192]{2,1,0:T(8,128)} %list_ref.1, s32[3,8]{1,0:T(4,128)} %count_ref.1, s32[3]{0:T(128)} %owner_ref.1, f32[1024,768]{1,0:T(8,128)} %cache_hbm.1, f32[512,768]{1,0:T(8,128)} %fresh_hbm.1), custom_call_target="tpu_custom_call" | custom-call | tf_op jit(solution)/shard_map/cache_step/pallas_call | solution.py:421
  120.5 1.7 %copy.11 = f32[3,32,768]{2,1,0:T(8,128)} copy(f32[3,32,768]{2,1,0:T(8,128)} %get-tuple-element.4) | data formatting | bytes 589824
  122.2 3.8 %copy.12 = f32[1024,768]{1,0:T(8,128)} copy(f32[1024,768]{1,0:T(8,128)} %get-tuple-element.5) | data formatting | bytes 6291456

commit v2 on v1

--- a/solution.py
+++ b/solution.py
@@ -31,7 +31,7 @@
 def kernel(
     q_hbm, pos_ref, list_ref, count_ref, owner_ref, cache_hbm, fresh_hbm,
     qg_hbm, cg_hbm,
-    q, chi, clo, e, zs, ah, al, mloc, keep, factor, factor_w, posx, lse,
+    q, chi, clo, e, zs, ah, al, dh, dl, mloc, keep, factor, factor_w, posx, lse,
     stat_out, stat_in, t, r1, u, r2, r3, g, pair_in, far_in,
     in_sem, out_sem, send_sem, recv_sem,
 ):
@@ -155,26 +155,28 @@
 
     def scores(s, begin, count):
         @pl.loop(begin, begin + count)
-        def _(a):
-            c = s * RING + a
-            block_q = q[s, pl.ds(pl.multiple_of(a * rows, rows), rows), :]
+        def _(h):
+            block_q = q[s, pl.ds(pl.multiple_of(h * 2 * rows, 2 * rows), 2 * rows), :]
             zs[...] = mm(chi[s], block_q, NT) + mm(clo[s], block_q, NT)
-            sums = []
-            for j in range(blocks):
-                at = slice(j * BLK, (j + 1) * BLK)
-                z = zs[at, :]
-                peak = jnp.max(z, axis=0, keepdims=True)
-                value = jnp.exp2((z - peak) * (scale * log2e))
-                e[c, at, :] = value
-                mloc[c, j:j + 1, :] = peak * scale
-                sums.append(jnp.sum(value, axis=0, keepdims=True))
-            w = weights(s, c)
-            peaks = jnp.where(w > 0.0, mloc[c], NEG)
-            top = jnp.max(peaks, axis=0, keepdims=True)
-            total = jnp.concatenate(sums, axis=0) * jnp.exp(peaks - top)
-            total = jnp.sum(jnp.where(w > 0.0, w * total, 0.0), axis=0, keepdims=True)
-            stat_out[s, 0, pl.ds(a, 1), :] = top
-            stat_out[s, 0, pl.ds(RING + a, 1), :] = total
+            for i in range(2):
+                a = 2 * h + i
+                c = s * RING + a
+                sums = []
+                for j in range(blocks):
+                    at = slice(j * BLK, (j + 1) * BLK)
+                    z = zs[at, i * rows:(i + 1) * rows]
+                    peak = jnp.max(z, axis=0, keepdims=True)
+                    value = jnp.exp2((z - peak) * (scale * log2e))
+                    e[c, at, :] = value
+                    mloc[c, j:j + 1, :] = peak * scale
+                    sums.append(jnp.sum(value, axis=0, keepdims=True))
+                w = weights(s, c)
+                peaks = jnp.where(w > 0.0, mloc[c], NEG)
+                top = jnp.max(peaks, axis=0, keepdims=True)
+                total = jnp.concatenate(sums, axis=0) * jnp.exp(peaks - top)
+                total = jnp.sum(jnp.where(w > 0.0, w * total, 0.0), axis=0, keepdims=True)
+                stat_out[s, 0, pl.ds(a, 1), :] = top
+                stat_out[s, 0, pl.ds(RING + a, 1), :] = total
 
     def stat_copy(s, stage):
         base = s * 7 + stage * 3
@@ -225,8 +227,8 @@
         copy.start()
         sent.append(copy)
 
-    def terms(s):
-        @pl.loop(0, RING)
+    def terms(s, begin, end):
+        @pl.loop(begin, end)
         def _(k):
             hop = jnp.where(k == 0, 2, jnp.where(k == 1, 1, jnp.where(k == 2, 3, 0)))
             a = (own_a + hop) % RING
@@ -254,7 +256,8 @@
             def _():
                 ring1(s, 4).start()
 
-        sent.extend(ring1(s, i) for i in (0, 1, 2, 4))
+        if end == RING:
+            sent.extend(ring1(s, i) for i in (0, 1, 2, 4))
 
     def relay1(s):
         ring1(s, 0).wait_recv()
@@ -312,96 +315,123 @@
     def out_copy(s):
         return pltpu.make_async_copy(piece(s, 0, zl), qg_hbm.at[s], out_sem.at[s])
 
-    side_rows = cols // 2
-    other_at = pl.ds(pl.multiple_of((1 - core) * side_rows, side_rows), side_rows)
-    mine_at = pl.ds(pl.multiple_of(core * side_rows, side_rows), side_rows)
+    side = cols // 2
+    pieces = side // BLK
     base = 21 + steps * 13
-    pair_copy = remote(base, g.at[other_at], pair_in, pair_peer)
-    far_copy = remote(base + 1, g.at[mine_at], far_in, far_peer)
-    final_copy = remote(base + 2, g.at[mine_at], cg_hbm.at[mine_at], pair_peer)
-    final_local = pltpu.make_async_copy(g.at[mine_at], cg_hbm.at[mine_at], out_sem.at[steps])
-
-    def gradient(side, at):
-        g[at, :] = jnp.zeros((side_rows, width), F32)
-
-        @pl.loop(0, steps * RING)
-        def _(c):
-            s, a = c // RING, c % RING
-            for j in range(side_rows // BLK):
-                where = pl.ds(pl.multiple_of(side * side_rows, side_rows) + j * BLK, BLK)
-                scaled = factor[c, pl.ds(side * (side_rows // BLK) + j, 1), :]
-                put = slice(j * BLK, (j + 1) * BLK)
-                ah[put, :], al[put, :] = halves(e[c, where, :] * scaled)
-            block_q = q[s, pl.ds(pl.multiple_of(a * rows, rows), rows), :]
-            g[at, :] += mm(ah[:side_rows, :], block_q, NN) + mm(al[:side_rows, :], block_q, NN)
-
+
+    def spot(which, p):
+        return pl.ds(pl.multiple_of(which * side + p * BLK, BLK), BLK)
+
+    def pair_copy(p):
+        return remote(base + p, g.at[spot(1 - core, p)], pair_in.at[p], pair_peer)
+
+    def far_copy(p):
+        return remote(base + pieces + p, g.at[spot(core, p)], far_in.at[p], far_peer)
+
+    def final_copy(p):
+        at = spot(core, p)
+        return remote(base + 2 * pieces + p, g.at[at], cg_hbm.at[at], pair_peer)
+
+    def final_local(p):
+        at = spot(core, p)
+        return pltpu.make_async_copy(g.at[at], cg_hbm.at[at], out_sem.at[steps + p])
+
+    def gradient(p):
+        for i, which in enumerate((1 - core, core)):
+            for c in range(steps * RING):
+                scaled = factor[c, pl.ds(which * pieces + p, 1), :]
+                put = (slice(i * BLK, (i + 1) * BLK), slice(c * rows, (c + 1) * rows))
+                dh[put], dl[put] = halves(e[c, spot(which, p), :] * scaled)
+        every = q[...].reshape(steps * RING * rows, width)
+        both = mm(dh[...], every, NN) + mm(dl[...], every, NN)
+        g[spot(1 - core, p), :] = both[:BLK]
+        g[spot(core, p), :] = both[BLK:]
+        start(pair_copy(p))
+
+    def pair_add(p):
+        pair_copy(p).wait_recv()
+        g[spot(core, p), :] += pair_in[p]
+        far_copy(p).start()
+
+    def far_add(p):
+        far_copy(p).wait()
+        g[spot(core, p), :] += far_in[p]
+        final_copy(p).start()
+        final_local(p).start()
+
+    def q_ready(s):
+        pltpu.make_async_copy(q_hbm.at[s], q.at[s], in_sem.at[q_sem + s]).wait()
+
+    for s in range(steps):
+        tables(s)
     load_c.wait()
     for load in loads_f:
         load.wait()
     prepare()
-    for s in range(steps):
-        tables(s)
-
-    def q_ready(s):
-        pltpu.make_async_copy(q_hbm.at[s], q.at[s], in_sem.at[q_sem + s]).wait()
 
     q_ready(0)
-    scores(0, 0, RING)
+    scores(0, 0, 2)
     pl.semaphore_wait(barrier, len(peers))
     stat_send(0, 0)
     q_ready(1)
-    scores(1, 0, 2)
+    scores(1, 0, 1)
     stat_merge(0, 0)
-    scores(1, 2, 2)
+    scores(1, 1, 1)
+    stat_send(1, 0)
     stat_merge(0, 1)
-    stat_send(1, 0)
     q_ready(2)
     scores(2, 0, 1)
     stat_merge(0, 2)
-    terms(0)
     stat_merge(1, 0)
+    terms(0, 0, 1)
     scores(2, 1, 1)
+    stat_send(2, 0)
     stat_merge(1, 1)
+    terms(0, 1, 3)
+    stat_merge(1, 2)
+    stat_merge(2, 0)
+    terms(0, 3, 4)
+    stat_merge(2, 1)
     relay1(0)
-    scores(2, 2, 2)
-    stat_send(2, 0)
-    stat_merge(1, 2)
-    terms(1)
-    stat_merge(2, 0)
+    terms(1, 0, 1)
+    stat_merge(2, 2)
+    gradient(0)
+    terms(1, 1, 2)
+    pair_add(0)
+    terms(1, 2, 4)
     finish1(0)
+    gradient(1)
     relay1(1)
-    stat_merge(2, 1)
     relay2(0)
-    stat_merge(2, 2)
-    gradient(1 - core, other_at)
-    pair_copy.start()
-    terms(2)
+    terms(2, 0, 2)
+    pair_add(1)
     finish2(0)
+    terms(2, 2, 4)
+    finish3(0)
+    gradient(2)
     finish1(1)
+    pair_add(2)
+    gradient(3)
     relay1(2)
-    finish3(0)
     relay2(1)
-    gradient(core, mine_at)
-    pair_copy.wait_recv()
-    g[mine_at, :] += pair_in[...]
-    far_copy.start()
+    pair_add(3)
+    far_add(0)
     finish2(1)
+    far_add(1)
+    finish3(1)
+    far_add(2)
     finish1(2)
-    finish3(1)
     relay2(2)
     finish2(2)
     finish3(2)
-    far_copy.wait()
-    g[mine_at, :] += far_in[...]
-    final_copy.start()
-    final_local.start()
+    far_add(3)
     for copy in sent:
         copy.wait_send()
-    pair_copy.wait_send()
     for s in range(steps):
         out_copy(s).wait()
-    final_local.wait()
-    final_copy.wait()
+    for p in range(pieces):
+        final_local(p).wait()
+        final_copy(p).wait()
 
 
 def on_device(queries, positives, block_list, block_count, refresh_owner, cache, fresh):
@@ -413,7 +443,8 @@
     chunks = steps * RING
     blocks = cols // BLK
     half, part = rows // 2, rows // RING // 2
-    messages = 21 + steps * 13 + 3
+    pieces = cols // 2 // BLK
+    messages = 21 + steps * 13 + 3 * pieces
     vmem = pl.BlockSpec(memory_space=pltpu.VMEM)
     smem = pl.BlockSpec(memory_space=pltpu.SMEM)
     anywhere = pl.BlockSpec(memory_space=pl.ANY)
@@ -431,9 +462,11 @@
             pltpu.VMEM((steps, cols, width), BF16),
             pltpu.VMEM((steps, cols, width), BF16),
             pltpu.VMEM((chunks, cols, rows), F32),
-            pltpu.VMEM((cols, rows), F32),
+            pltpu.VMEM((cols, 2 * rows), F32),
             pltpu.VMEM((cols, rows), BF16),
             pltpu.VMEM((cols, rows), BF16),
+            pltpu.VMEM((2 * BLK, chunks * rows), BF16),
+            pltpu.VMEM((2 * BLK, chunks * rows), BF16),
             small, small, small, small,
             pltpu.VMEM((chunks, 8, rows), jnp.int32),
             pltpu.VMEM((steps, 8, rows), F32),
@@ -445,10 +478,10 @@
             pltpu.VMEM((steps, 6, part, width), F32),
             pltpu.VMEM((steps, part, width), F32),
             pltpu.VMEM((cols, width), F32),
-            pltpu.VMEM((cols // 2, width), F32),
-            pltpu.VMEM((cols // 2, width), F32),
+            pltpu.VMEM((pieces, BLK, width), F32),
+            pltpu.VMEM((pieces, BLK, width), F32),
             pltpu.SemaphoreType.DMA((1 + fresh.shape[0] // rows + steps,)),
-            pltpu.SemaphoreType.DMA((steps + 1,)),
+            pltpu.SemaphoreType.DMA((steps + pieces,)),
             pltpu.SemaphoreType.DMA((messages,)),
             pltpu.SemaphoreType.DMA((messages,)),
         ],

time: 127 us -> 115 us (0.906)
  Pallas kernels: 120 us -> 107 us
    pallas_call x1, Pallas kernels: 120 us -> 107 us  [on_device(): pl.pallas_call(kernel, out_shape=(jax.ShapeDtypeStruct((steps, share, wid...]
where the time goes in v2:
time: 115 us; the launch traced here: 113 us
  Pallas kernels  107 us (93%)
  local copies, waits for them, and re-layouts  5.45 us (5%)
    pallas_call x1, Pallas kernels, on_device(): pl.pallas_call(kernel, out_shape=(jax.ShapeDtypeStruct((steps, share, wid...  107 us
    unnamed x2, local copies, waits for them, and re-layouts  5.45 us

profile of v2, /device:TPU:0, one launch (start us, length us, event | category | flops | bytes accessed | tf_op | source)
XLA Modules:
  0.0 113.5 jit_solution(13622590282330337113)
XLA Ops:
  0.6 107.4 %cache_step.1 = (f32[3,32,768]{2,1,0:T(8,128)}, f32[1024,768]{1,0:T(8,128)}) custom-call(bf16[3,1024,768]{2,1,0:T(8,128)(2,1)} %q_hbm.1, s32[3,1024]{1,0:T(4,128)} %pos_ref.1, s32[3,8,192]{2,1,0:T(8,128)} %list_ref.1, s32[3,8]{1,0:T(4,128)} %count_ref.1, s32[3]{0:T(128)} %owner_ref.1, f32[1024,768]{1,0:T(8,128)} %cache_hbm.1, f32[512,768]{1,0:T(8,128)} %fresh_hbm.1), custom_call_target="tpu_custom_call" | custom-call | tf_op jit(solution)/shard_map/cache_step/pallas_call | solution.py:452
  108.0 1.7 %copy.11 = f32[3,32,768]{2,1,0:T(8,128)} copy(f32[3,32,768]{2,1,0:T(8,128)} %get-tuple-element.4) | data formatting | bytes 589824
  109.7 3.8 %copy.12 = f32[1024,768]{1,0:T(8,128)} copy(f32[1024,768]{1,0:T(8,128)} %get-tuple-element.5) | data formatting | bytes 6291456

commit v3 on v2

--- a/solution.py
+++ b/solution.py
@@ -63,10 +63,15 @@
     def second(d):
         return (((x + d * two) % 4) * 8 + ((y + d * one) % 4) * 2 + zl, bi)
 
-    z_peer = (ci + 1 - 2 * zl, bi)
+    def flip(device):
+        return (device[0] + 1 - 2 * zl, device[1])
+
+    z_peer = flip((ci, bi))
     far_peer = (ci, (1 - zh) * 2 + core)
     pair_peer = (ci, zh * 2 + 1 - core)
-    peers = [first(1), first(2), first(3), second(1), second(2), second(3), z_peer, far_peer, pair_peer]
+    near = [second(1), second(2), second(3), z_peer, flip(second(1)), flip(second(2)), flip(second(3))]
+    across = [first(1), first(2), first(3)]
+    peers = near + across + [far_peer, pair_peer]
 
     def remote(number, src, dst, device):
         return pltpu.make_async_remote_copy(
@@ -74,6 +79,8 @@
             device_id=device, device_id_type=pl.DeviceIdType.MESH,
         )
 
+    stat_messages = len(near) + len(across)
+    base0 = steps * stat_messages
     barrier = pltpu.get_barrier_semaphore()
     for peer in peers:
         pl.semaphore_signal(barrier, inc=1, device_id=peer, device_id_type=pl.DeviceIdType.MESH)
@@ -85,9 +92,10 @@
         loads_f.append(pltpu.make_async_copy(fresh_hbm.at[pl.ds(i * rows, rows)], u.at[i], in_sem.at[1 + i]))
         loads_f[-1].start()
     q_sem = 1 + slab // rows
-    for s in range(steps):
+
+    def load_q(s):
         @pl.loop(0, RING * RING)
-        def _(i, s=s):
+        def _(i):
             a, b = i // RING, i % RING
             src = (a * one + b * two) * rows + (b * one + a * two) * quarter
             pltpu.make_async_copy(
@@ -95,6 +103,8 @@
                 q.at[s, pl.ds(pl.multiple_of(i * quarter, quarter), quarter)],
                 in_sem.at[q_sem + s],
             ).start()
+
+    load_q(0)
 
     lanes = lax.broadcasted_iota(jnp.int32, (blocks, rows), 1)
     slot = lax.broadcasted_iota(jnp.int32, (1, list_width), 1)
@@ -131,12 +141,12 @@
         top = lax.broadcasted_iota(jnp.int32, (blocks, rows), 0) < slab_blocks
         return keep[c] + jnp.where(mine & top, 1.0, 0.0)
 
-    def prepare():
-        @pl.loop(0, cols // BLK)
+    def prepare(begin, end):
+        @pl.loop(slab // BLK, cols // BLK)
         def _(i):
             at = pl.ds(pl.multiple_of(i * BLK, BLK), BLK)
             high, low = halves(g[at, :])
-            for s in range(steps):
+            for s in range(begin, end):
                 chi[s, at, :] = high
                 clo[s, at, :] = low
 
@@ -147,50 +157,46 @@
             old = g[at, :]
             new = u[i // per, pl.ds(pl.multiple_of((i % per) * BLK, BLK), BLK), :]
             done = jnp.zeros((BLK, width), jnp.bool_)
-            for s in range(steps):
+            for s in range(end):
                 done = done | (jnp.broadcast_to(owner_ref[s], (BLK, width)) == ci)
-                high, low = halves(jnp.where(done, new, old))
-                chi[s, at, :] = high
-                clo[s, at, :] = low
-
-    def scores(s, begin, count):
-        @pl.loop(begin, begin + count)
-        def _(h):
-            block_q = q[s, pl.ds(pl.multiple_of(h * 2 * rows, 2 * rows), 2 * rows), :]
-            zs[...] = mm(chi[s], block_q, NT) + mm(clo[s], block_q, NT)
-            for i in range(2):
-                a = 2 * h + i
-                c = s * RING + a
-                sums = []
-                for j in range(blocks):
-                    at = slice(j * BLK, (j + 1) * BLK)
-                    z = zs[at, i * rows:(i + 1) * rows]
-                    peak = jnp.max(z, axis=0, keepdims=True)
-                    value = jnp.exp2((z - peak) * (scale * log2e))
-                    e[c, at, :] = value
-                    mloc[c, j:j + 1, :] = peak * scale
-                    sums.append(jnp.sum(value, axis=0, keepdims=True))
-                w = weights(s, c)
-                peaks = jnp.where(w > 0.0, mloc[c], NEG)
-                top = jnp.max(peaks, axis=0, keepdims=True)
-                total = jnp.concatenate(sums, axis=0) * jnp.exp(peaks - top)
-                total = jnp.sum(jnp.where(w > 0.0, w * total, 0.0), axis=0, keepdims=True)
-                stat_out[s, 0, pl.ds(a, 1), :] = top
-                stat_out[s, 0, pl.ds(RING + a, 1), :] = total
+                if s >= begin:
+                    high, low = halves(jnp.where(done, new, old))
+                    chi[s, at, :] = high
+                    clo[s, at, :] = low
+
+    def scores(s, h):
+        block_q = q[s, pl.ds(pl.multiple_of(h * 2 * rows, 2 * rows), 2 * rows), :]
+        zs[...] = mm(chi[s], block_q, NT) + mm(clo[s], block_q, NT)
+        for i in range(2):
+            a = 2 * h + i
+            c = s * RING + a
+            sums = []
+            for j in range(blocks):
+                at = slice(j * BLK, (j + 1) * BLK)
+                z = zs[at, i * rows:(i + 1) * rows]
+                peak = jnp.max(z, axis=0, keepdims=True)
+                value = jnp.exp2((z - peak) * (scale * log2e))
+                e[c, at, :] = value
+                mloc[c, j:j + 1, :] = peak * scale
+                sums.append(jnp.sum(value, axis=0, keepdims=True))
+            w = weights(s, c)
+            peaks = jnp.where(w > 0.0, mloc[c], NEG)
+            top = jnp.max(peaks, axis=0, keepdims=True)
+            total = jnp.concatenate(sums, axis=0) * jnp.exp(peaks - top)
+            total = jnp.sum(jnp.where(w > 0.0, w * total, 0.0), axis=0, keepdims=True)
+            stat_out[s, 0, pl.ds(a, 1), :] = top
+            stat_out[s, 0, pl.ds(RING + a, 1), :] = total
 
     def stat_copy(s, stage):
-        base = s * 7 + stage * 3
-        if stage == 2:
-            return [remote(base, stat_out.at[s, 2], stat_in.at[s, 2, 0], z_peer)]
-        where = first if stage == 0 else second
-        return [remote(base + d - 1, stat_out.at[s, stage], stat_in.at[s, stage, d - 1], where(d)) for d in (1, 2, 3)]
-
-    sent = []
+        base = s * stat_messages + stage * len(near)
+        return [
+            remote(base + i, stat_out.at[s, stage], stat_in.at[s, stage, i], device)
+            for i, device in enumerate(across if stage else near)
+        ]
 
     def stat_send(s, stage):
         for copy in stat_copy(s, stage):
             copy.start()
-            sent.append(copy)
 
     def stat_merge(s, stage):
         copies = stat_copy(s, stage)
@@ -200,10 +206,10 @@
         tops = [v[:RING] for v in got]
         top = functools.reduce(jnp.maximum, tops)
         total = sum(v[RING:] * jnp.exp(p - top) for v, p in zip(got, tops))
-        if stage < 2:
-            stat_out[s, stage + 1, :RING, :] = top
-            stat_out[s, stage + 1, RING:, :] = total
-            stat_send(s, stage + 1)
+        if stage == 0:
+            stat_out[s, 1, :RING, :] = top
+            stat_out[s, 1, RING:, :] = total
+            stat_send(s, 1)
             return
         lse[s, :RING, :] = top + jnp.log(total)
         for a in range(RING):
@@ -221,51 +227,33 @@
             (t.at[s, 1, high], right), (t.at[s, 1, low], right),
             (t.at[s, 2, low], left), (t.at[s, 2, high], left),
         ][i]
-        return remote(21 + s * 13 + i, src, r1.at[s, i], device)
-
-    def start(copy):
-        copy.start()
-        sent.append(copy)
-
-    def terms(s, begin, end):
-        @pl.loop(begin, end)
-        def _(k):
-            hop = jnp.where(k == 0, 2, jnp.where(k == 1, 1, jnp.where(k == 2, 3, 0)))
-            a = (own_a + hop) % RING
-            c = s * RING + a
-            place = posx[c, 0:1, :]
-            for j in range(blocks):
-                at = slice(j * BLK, (j + 1) * BLK)
-                value = e[c, at, :] * factor_w[c, j:j + 1, :]
-                if j < slab_blocks:
-                    row = lax.broadcasted_iota(jnp.int32, (BLK, rows), 0) + j * BLK
-                    value = value - jnp.where(row == place, 1.0, 0.0)
-                ah[at, :], al[at, :] = halves(value)
-            t[s, k] = mm(ah[...], chi[s], TN) + mm(ah[...], clo[s], TN) + mm(al[...], chi[s], TN)
-
-            @pl.when(k == 0)
-            def _():
-                ring1(s, 0).start()
-                ring1(s, 1).start()
-
-            @pl.when(k == 1)
-            def _():
-                ring1(s, 2).start()
-
-            @pl.when(k == 2)
-            def _():
-                ring1(s, 4).start()
-
-        if end == RING:
-            sent.extend(ring1(s, i) for i in (0, 1, 2, 4))
+        return remote(base0 + s * 13 + i, src, r1.at[s, i], device)
+
+    def terms(s, k):
+        hop = jnp.where(k == 0, 2, jnp.where(k == 1, 1, jnp.where(k == 2, 3, 0)))
+        a = (own_a + hop) % RING
+        c = s * RING + a
+        place = posx[c, 0:1, :]
+        for j in range(blocks):
+            at = slice(j * BLK, (j + 1) * BLK)
+            value = e[c, at, :] * factor_w[c, j:j + 1, :]
+            if j < slab_blocks:
+                row = lax.broadcasted_iota(jnp.int32, (BLK, rows), 0) + j * BLK
+                value = value - jnp.where(row == place, 1.0, 0.0)
+            ah[at, :], al[at, :] = halves(value)
+        t[s, k] = mm(ah[...], chi[s], TN) + mm(ah[...], clo[s], TN) + mm(al[...], chi[s], TN)
+
+    def push(s, *which):
+        for i in which:
+            ring1(s, i).start()
 
     def relay1(s):
         ring1(s, 0).wait_recv()
         t[s, 1, :half, :] += r1[s, 0]
-        start(ring1(s, 3))
+        ring1(s, 3).start()
         ring1(s, 1).wait_recv()
         t[s, 2, half:, :] += r1[s, 1]
-        start(ring1(s, 5))
+        ring1(s, 5).start()
 
     def piece(s, d, side):
         at = ((own_b + d) % RING) * quarter + side * part
@@ -274,7 +262,7 @@
     def ring2(s, i):
         right, left = second(1), second(3)
         d, side, device = [(2, 0, right), (2, 1, left), (1, 1, right), (1, 0, right), (3, 0, left), (3, 1, left)][i]
-        return remote(21 + s * 13 + 6 + i, piece(s, d, side), r2.at[s, i], device)
+        return remote(base0 + s * 13 + 6 + i, piece(s, d, side), r2.at[s, i], device)
 
     def finish1(s):
         for i in (2, 3, 4, 5):
@@ -282,20 +270,20 @@
         u[s, :half, :] = t[s, 3, :half, :] + r1[s, 3] + r1[s, 4]
         u[s, half:, :] = t[s, 3, half:, :] + r1[s, 2] + r1[s, 5]
         for i in (0, 1, 2, 4):
-            start(ring2(s, i))
+            ring2(s, i).start()
 
     def relay2(s):
         ring2(s, 0).wait_recv()
         ref = piece(s, 1, 0)
         ref[...] += r2[s, 0]
-        start(ring2(s, 3))
+        ring2(s, 3).start()
         ring2(s, 1).wait_recv()
         ref = piece(s, 3, 1)
         ref[...] += r2[s, 1]
-        start(ring2(s, 5))
+        ring2(s, 5).start()
 
     def last(s):
-        return remote(21 + s * 13 + 12, piece(s, 0, 1 - zl), r3.at[s], z_peer)
+        return remote(base0 + s * 13 + 12, piece(s, 0, 1 - zl), r3.at[s], z_peer)
 
     def finish2(s):
         for i in (2, 3, 4, 5):
@@ -304,7 +292,7 @@
         ref[...] += r2[s, 3] + r2[s, 4]
         ref = piece(s, 0, 1)
         ref[...] += r2[s, 2] + r2[s, 5]
-        start(last(s))
+        last(s).start()
 
     def finish3(s):
         last(s).wait_recv()
@@ -317,7 +305,7 @@
 
     side = cols // 2
     pieces = side // BLK
-    base = 21 + steps * 13
+    base = base0 + steps * 13
 
     def spot(which, p):
         return pl.ds(pl.multiple_of(which * side + p * BLK, BLK), BLK)
@@ -336,7 +324,7 @@
         at = spot(core, p)
         return pltpu.make_async_copy(g.at[at], cg_hbm.at[at], out_sem.at[steps + p])
 
-    def gradient(p):
+    def gradient(p, _):
         for i, which in enumerate((1 - core, core)):
             for c in range(steps * RING):
                 scaled = factor[c, pl.ds(which * pieces + p, 1), :]
@@ -346,7 +334,7 @@
         both = mm(dh[...], every, NN) + mm(dl[...], every, NN)
         g[spot(1 - core, p), :] = both[:BLK]
         g[spot(core, p), :] = both[BLK:]
-        start(pair_copy(p))
+        pair_copy(p).start()
 
     def pair_add(p):
         pair_copy(p).wait_recv()
@@ -362,76 +350,107 @@
     def q_ready(s):
         pltpu.make_async_copy(q_hbm.at[s], q.at[s], in_sem.at[q_sem + s]).wait()
 
-    for s in range(steps):
-        tables(s)
+    tables(0)
     load_c.wait()
     for load in loads_f:
         load.wait()
-    prepare()
-
+    for s in range(1, steps):
+        load_q(s)
+    prepare(0, 1)
     q_ready(0)
-    scores(0, 0, 2)
     pl.semaphore_wait(barrier, len(peers))
-    stat_send(0, 0)
-    q_ready(1)
-    scores(1, 0, 1)
-    stat_merge(0, 0)
-    scores(1, 1, 1)
-    stat_send(1, 0)
-    stat_merge(0, 1)
-    q_ready(2)
-    scores(2, 0, 1)
-    stat_merge(0, 2)
-    stat_merge(1, 0)
-    terms(0, 0, 1)
-    scores(2, 1, 1)
-    stat_send(2, 0)
-    stat_merge(1, 1)
-    terms(0, 1, 3)
-    stat_merge(1, 2)
-    stat_merge(2, 0)
-    terms(0, 3, 4)
-    stat_merge(2, 1)
-    relay1(0)
-    terms(1, 0, 1)
-    stat_merge(2, 2)
-    gradient(0)
-    terms(1, 1, 2)
-    pair_add(0)
-    terms(1, 2, 4)
-    finish1(0)
-    gradient(1)
-    relay1(1)
-    relay2(0)
-    terms(2, 0, 2)
-    pair_add(1)
-    finish2(0)
-    terms(2, 2, 4)
-    finish3(0)
-    gradient(2)
-    finish1(1)
-    pair_add(2)
-    gradient(3)
-    relay1(2)
-    relay2(1)
+
+    plan = [
+        ("s", 0, 0, []),
+        ("s", 0, 1, [(stat_send, 0, 0), (prepare, 1, steps), (tables, 1), (tables, 2), (q_ready, 1), (q_ready, 2)]),
+        ("s", 1, 0, [(stat_merge, 0, 0)]),
+        ("s", 1, 1, [(stat_send, 1, 0), (stat_merge, 0, 1)]),
+        ("t", 0, 0, [(push, 0, 0, 1)]),
+        ("s", 2, 0, [(stat_merge, 1, 0)]),
+        ("s", 2, 1, [(stat_send, 2, 0)]),
+        ("t", 0, 1, [(stat_merge, 2, 0), (push, 0, 2), (stat_merge, 1, 1)]),
+        ("t", 0, 2, [(push, 0, 4)]),
+        ("t", 0, 3, [(relay1, 0), (stat_merge, 2, 1)]),
+        ("g", 0, 0, []),
+        ("t", 1, 0, [(push, 1, 0, 1), (pair_add, 0)]),
+        ("t", 1, 1, [(push, 1, 2)]),
+        ("t", 1, 2, [(push, 1, 4)]),
+        ("g", 1, 0, [(finish1, 0)]),
+        ("t", 1, 3, [(relay1, 1), (pair_add, 1)]),
+        ("t", 2, 0, [(push, 2, 0, 1), (relay2, 0)]),
+        ("t", 2, 1, [(push, 2, 2)]),
+        ("g", 2, 0, []),
+        ("t", 2, 2, [(push, 2, 4), (finish2, 0), (pair_add, 2)]),
+        ("t", 2, 3, []),
+        ("g", 3, 0, [(finish1, 1)]),
+    ]
+
+    @pl.loop(0, len(plan))
+    def _(n):
+        for name, work in (("s", scores), ("t", terms), ("g", gradient)):
+            mine = [(i, entry) for i, entry in enumerate(plan) if entry[0] == name]
+
+            @pl.when(functools.reduce(jnp.logical_or, [n == i for i, _ in mine]))
+            def _(mine=mine, work=work):
+                work(sum(jnp.where(n == i, entry[1], 0) for i, entry in mine), sum(jnp.where(n == i, entry[2], 0) for i, entry in mine))
+
+        for i, entry in enumerate(plan):
+            if entry[3]:
+                @pl.when(n == i)
+                def _(todo=entry[3]):
+                    for call, *args in todo:
+                        call(*args)
+
     pair_add(3)
     far_add(0)
+    relay2(1)
+    relay1(2)
+    far_add(1)
     finish2(1)
-    far_add(1)
-    finish3(1)
+    finish3(0)
     far_add(2)
     finish1(2)
     relay2(2)
+    finish3(1)
     finish2(2)
+    far_add(3)
     finish3(2)
-    far_add(3)
-    for copy in sent:
-        copy.wait_send()
     for s in range(steps):
+        for stage in range(2):
+            for copy in stat_copy(s, stage):
+                copy.wait_send()
+        for i in range(6):
+            ring1(s, i).wait_send()
+            ring2(s, i).wait_send()
+        last(s).wait_send()
         out_copy(s).wait()
     for p in range(pieces):
+        pair_copy(p).wait_send()
         final_local(p).wait()
         final_copy(p).wait()
+
+
+def publish(a_ref, b_ref, a_out, b_out, a_buf, b_buf, sems):
+    tiles = b_ref.shape[0] // BLK
+
+    def moves(src, buf, dst):
+        def at(i):
+            return pl.ds(i * BLK, BLK)
+
+        first = [pltpu.make_async_copy(src.at[at(i)], buf.at[at(i)], sems.at[0, i]) for i in range(tiles)]
+        second = [pltpu.make_async_copy(buf.at[at(i)], dst.at[at(i)], sems.at[1, i]) for i in range(tiles)]
+        return first, second
+
+    first, second = moves(b_ref, b_buf, b_out)
+    first.append(pltpu.make_async_copy(a_ref, a_buf, sems.at[0, tiles]))
+    second.append(pltpu.make_async_copy(a_buf, a_out, sems.at[1, tiles]))
+    for copy in first:
+        copy.start()
+    for one, two in zip(first, second):
+        one.wait()
+        two.start()
+    for copy in second:
+        copy.wait()
 
 
 def on_device(queries, positives, block_list, block_count, refresh_owner, cache, fresh):
@@ -444,12 +463,12 @@
     blocks = cols // BLK
     half, part = rows // 2, rows // RING // 2
     pieces = cols // 2 // BLK
-    messages = 21 + steps * 13 + 3 * pieces
+    messages = steps * 23 + 3 * pieces
     vmem = pl.BlockSpec(memory_space=pltpu.VMEM)
     smem = pl.BlockSpec(memory_space=pltpu.SMEM)
     anywhere = pl.BlockSpec(memory_space=pl.ANY)
     small = pltpu.VMEM((chunks, blocks, rows), F32)
-    return pl.pallas_call(
+    a, b = pl.pallas_call(
         kernel,
         out_shape=(
             jax.ShapeDtypeStruct((steps, share, width), F32),
@@ -470,8 +489,8 @@
             small, small, small, small,
             pltpu.VMEM((chunks, 8, rows), jnp.int32),
             pltpu.VMEM((steps, 8, rows), F32),
-            pltpu.VMEM((steps, 3, 8, rows), F32),
-            pltpu.VMEM((steps, 3, 3, 8, rows), F32),
+            pltpu.VMEM((steps, 2, 8, rows), F32),
+            pltpu.VMEM((steps, 2, 7, 8, rows), F32),
             pltpu.VMEM((steps, RING, rows, width), F32),
             pltpu.VMEM((steps, 6, half, width), F32),
             pltpu.VMEM((steps, rows, width), F32),
@@ -490,6 +509,18 @@
         ),
         name="cache_step",
     )(queries, positives, block_list, block_count, refresh_owner, cache, fresh)
+    return pl.pallas_call(
+        publish,
+        out_shape=(jax.ShapeDtypeStruct(a.shape, F32), jax.ShapeDtypeStruct(b.shape, F32)),
+        in_specs=[anywhere, anywhere],
+        out_specs=(anywhere, anywhere),
+        scratch_shapes=[
+            pltpu.VMEM(a.shape, F32),
+            pltpu.VMEM(b.shape, F32),
+            pltpu.SemaphoreType.DMA((2, cols // BLK + 1)),
+        ],
+        name="publish",
+    )(a, b)
 
 
 def solution(mesh):

time: 115 us -> 91.3 us (0.79); the launches traced: 113 us -> 91.2 us
  Pallas kernels: 107 us -> 90.5 us
  local copies, waits for them, and re-layouts: 5.45 us -> 0 us
    pallas_call x1, Pallas kernels: 107 us -> 87.6 us  [on_device(): pl.pallas_call(kernel, out_shape=(jax.ShapeDtypeStruct((steps, share, wid...]
    unnamed x2 -> x0, local copies, waits for them, and re-layouts: 5.45 us -> none
    pallas_call x0 -> x1, Pallas kernels: none -> 2.9 us  [on_device(): pl.pallas_call(publish, out_shape=(jax.ShapeDtypeStruct(a.shape, F32), ja...]
where the time goes in v3:
time: 91.3 us; the launch traced here: 91.2 us
  Pallas kernels  90.5 us (99%)
    pallas_call x1, Pallas kernels, on_device(): pl.pallas_call(kernel, out_shape=(jax.ShapeDtypeStruct((steps, share, wid...  87.6 us
    pallas_call x1, Pallas kernels, on_device(): pl.pallas_call(publish, out_shape=(jax.ShapeDtypeStruct(a.shape, F32), ja...  2.9 us

profile of v3, /device:TPU:0, one launch (start us, length us, event | category | flops | bytes accessed | tf_op | source)
XLA Modules:
  0.0 91.2 jit_solution(4357390115097393887)
XLA Ops:
  0.6 87.6 %cache_step.1 = (f32[3,32,768]{2,1,0:T(8,128)}, f32[1024,768]{1,0:T(8,128)}) custom-call(bf16[3,1024,768]{2,1,0:T(8,128)(2,1)} %q_hbm.1, s32[3,1024]{1,0:T(4,128)} %pos_ref.1, s32[3,8,192]{2,1,0:T(8,128)} %list_ref.1, s32[3,8]{1,0:T(4,128)} %count_ref.1, s32[3]{0:T(128)} %owner_ref.1, f32[1024,768]{1,0:T(8,128)} %cache_hbm.1, f32[512,768]{1,0:T(8,128)} %fresh_hbm.1), custom_call_target="tpu_custom_call" | custom-call | tf_op jit(solution)/shard_map/cache_step/pallas_call | solution.py:471
  88.3 2.9 %publish.1 = (f32[3,32,768]{2,1,0:T(8,128)}, f32[1024,768]{1,0:T(8,128)}) custom-call(f32[3,32,768]{2,1,0:T(8,128)} %get-tuple-element.4.a_ref, f32[1024,768]{1,0:T(8,128)} %get-tuple-element.5.b_ref), custom_call_target="tpu_custom_call" | custom-call | tf_op jit(solution)/shard_map/publish/pallas_call | solution.py:512

commit v4 on v3

--- a/solution.py
+++ b/solution.py
@@ -29,7 +29,7 @@
 
 
 def kernel(
-    q_hbm, pos_ref, list_ref, count_ref, owner_ref, cache_hbm, fresh_hbm,
+    split, q_hbm, pos_ref, list_ref, count_ref, owner_ref, cache_hbm, fresh_hbm,
     qg_hbm, cg_hbm,
     q, chi, clo, e, zs, ah, al, dh, dl, mloc, keep, factor, factor_w, posx, lse,
     stat_out, stat_in, t, r1, u, r2, r3, g, pair_in, far_in,
@@ -47,6 +47,8 @@
     half = rows // 2
     list_width = list_ref.shape[2]
     scale = 2.0 / math.sqrt(width)
+    flows = [(s, pl.ds(0, width)) for s in range(steps - 1)]
+    flows += [(steps - 1, pl.ds(0, split)), (steps - 1, pl.ds(split, width - split))]
     log2e = math.log2(math.e)
 
     ci = lax.axis_index("cache")
@@ -104,7 +106,8 @@
                 in_sem.at[q_sem + s],
             ).start()
 
-    load_q(0)
+    for s in range(steps):
+        load_q(s)
 
     lanes = lax.broadcasted_iota(jnp.int32, (blocks, rows), 1)
     slot = lax.broadcasted_iota(jnp.int32, (1, list_width), 1)
@@ -164,7 +167,8 @@
                     chi[s, at, :] = high
                     clo[s, at, :] = low
 
-    def scores(s, h):
+    def scores(count):
+        s, h = count // 2, count % 2
         block_q = q[s, pl.ds(pl.multiple_of(h * 2 * rows, 2 * rows), 2 * rows), :]
         zs[...] = mm(chi[s], block_q, NT) + mm(clo[s], block_q, NT)
         for i in range(2):
@@ -219,17 +223,20 @@
             factor[c] = jnp.where(keep[c] > 0.0, scaled, 0.0)
             factor_w[c] = jnp.where(w > 0.0, w * scaled, 0.0)
 
-    def ring1(s, i):
+    def ring1(f, i):
+        s, along = flows[f]
+        number = base0 + f * 13 + i
+        if f == 0 and i in (3, 5, 6, 7):
+            along = pl.ds(0 if i < 6 else width // 2, width // 2)
+            if i >= 6:
+                number, i = base0 + len(flows) * 13 + 3 * (cols // 2 // BLK) + i - 6, 2 * i - 9
         right, left = first(1), first(3)
         low, high = pl.ds(0, half), pl.ds(half, half)
-        src, device = [
-            (t.at[s, 0, low], right), (t.at[s, 0, high], left),
-            (t.at[s, 1, high], right), (t.at[s, 1, low], right),
-            (t.at[s, 2, low], left), (t.at[s, 2, high], left),
-        ][i]
-        return remote(base0 + s * 13 + i, src, r1.at[s, i], device)
-
-    def terms(s, k):
+        k, side, device = [(0, low, right), (0, high, left), (1, high, right), (1, low, right), (2, low, left), (2, high, left)][i]
+        return remote(number, t.at[s, k, side, along], r1.at[s, i, :, along], device)
+
+    def terms(count):
+        s, k = count // RING, count % RING
         hop = jnp.where(k == 0, 2, jnp.where(k == 1, 1, jnp.where(k == 2, 3, 0)))
         a = (own_a + hop) % RING
         c = s * RING + a
@@ -243,69 +250,72 @@
             ah[at, :], al[at, :] = halves(value)
         t[s, k] = mm(ah[...], chi[s], TN) + mm(ah[...], clo[s], TN) + mm(al[...], chi[s], TN)
 
-    def push(s, *which):
+    def push(f, *which):
         for i in which:
-            ring1(s, i).start()
-
-    def relay1(s):
-        ring1(s, 0).wait_recv()
-        t[s, 1, :half, :] += r1[s, 0]
-        ring1(s, 3).start()
-        ring1(s, 1).wait_recv()
-        t[s, 2, half:, :] += r1[s, 1]
-        ring1(s, 5).start()
-
-    def piece(s, d, side):
+            ring1(f, i).start()
+
+    def add(target, *sources):
+        target[...] += functools.reduce(jnp.add, [source[...] for source in sources])
+
+    def relay1(f):
+        s, along = flows[f]
+        for i, k, side, out in ((0, 1, pl.ds(0, half), 3), (1, 2, pl.ds(half, half), 5)):
+            ring1(f, i).wait_recv()
+            add(t.at[s, k, side, along], r1.at[s, i, :, along])
+            ring1(f, out).start()
+
+    def piece(f, d, side):
+        s, along = flows[f]
         at = ((own_b + d) % RING) * quarter + side * part
-        return u.at[s, pl.ds(pl.multiple_of(at, part), part)]
-
-    def ring2(s, i):
+        return u.at[s, pl.ds(pl.multiple_of(at, part), part), along]
+
+    def ring2(f, i):
+        s, along = flows[f]
         right, left = second(1), second(3)
         d, side, device = [(2, 0, right), (2, 1, left), (1, 1, right), (1, 0, right), (3, 0, left), (3, 1, left)][i]
-        return remote(base0 + s * 13 + 6 + i, piece(s, d, side), r2.at[s, i], device)
-
-    def finish1(s):
+        return remote(base0 + f * 13 + 6 + i, piece(f, d, side), r2.at[s, i, :, along], device)
+
+    def finish1(f):
+        s, along = flows[f]
+        for i in (2, 3, 4, 5) if f else (2, 3, 4, 5, 6, 7):
+            ring1(f, i).wait_recv()
+        u[s, :half, along] = t[s, 3, :half, along] + r1[s, 3, :, along] + r1[s, 4, :, along]
+        u[s, half:, along] = t[s, 3, half:, along] + r1[s, 2, :, along] + r1[s, 5, :, along]
+        for i in (0, 1, 2, 4):
+            ring2(f, i).start()
+
+    def relay2(f):
+        s, along = flows[f]
+        for i, d, side, out in ((0, 1, 0, 3), (1, 3, 1, 5)):
+            ring2(f, i).wait_recv()
+            add(piece(f, d, side), r2.at[s, i, :, along])
+            ring2(f, out).start()
+
+    def last(f):
+        s, along = flows[f]
+        return remote(base0 + f * 13 + 12, piece(f, 0, 1 - zl), r3.at[s, :, along], z_peer)
+
+    def finish2(f):
+        s, along = flows[f]
         for i in (2, 3, 4, 5):
-            ring1(s, i).wait_recv()
-        u[s, :half, :] = t[s, 3, :half, :] + r1[s, 3] + r1[s, 4]
-        u[s, half:, :] = t[s, 3, half:, :] + r1[s, 2] + r1[s, 5]
-        for i in (0, 1, 2, 4):
-            ring2(s, i).start()
-
-    def relay2(s):
-        ring2(s, 0).wait_recv()
-        ref = piece(s, 1, 0)
-        ref[...] += r2[s, 0]
-        ring2(s, 3).start()
-        ring2(s, 1).wait_recv()
-        ref = piece(s, 3, 1)
-        ref[...] += r2[s, 1]
-        ring2(s, 5).start()
-
-    def last(s):
-        return remote(base0 + s * 13 + 12, piece(s, 0, 1 - zl), r3.at[s], z_peer)
-
-    def finish2(s):
-        for i in (2, 3, 4, 5):
-            ring2(s, i).wait_recv()
-        ref = piece(s, 0, 0)
-        ref[...] += r2[s, 3] + r2[s, 4]
-        ref = piece(s, 0, 1)
-        ref[...] += r2[s, 2] + r2[s, 5]
-        last(s).start()
-
-    def finish3(s):
-        last(s).wait_recv()
-        ref = piece(s, 0, zl)
-        ref[...] += r3[s]
-        out_copy(s).start()
-
-    def out_copy(s):
-        return pltpu.make_async_copy(piece(s, 0, zl), qg_hbm.at[s], out_sem.at[s])
+            ring2(f, i).wait_recv()
+        add(piece(f, 0, 0), r2.at[s, 3, :, along], r2.at[s, 4, :, along])
+        add(piece(f, 0, 1), r2.at[s, 2, :, along], r2.at[s, 5, :, along])
+        last(f).start()
+
+    def finish3(f):
+        s, along = flows[f]
+        last(f).wait_recv()
+        add(piece(f, 0, zl), r3.at[s, :, along])
+        out_copy(f).start()
+
+    def out_copy(f):
+        s, along = flows[f]
+        return pltpu.make_async_copy(piece(f, 0, zl), qg_hbm.at[s, :, along], out_sem.at[f])
 
     side = cols // 2
     pieces = side // BLK
-    base = base0 + steps * 13
+    base = base0 + len(flows) * 13
 
     def spot(which, p):
         return pl.ds(pl.multiple_of(which * side + p * BLK, BLK), BLK)
@@ -322,9 +332,9 @@
 
     def final_local(p):
         at = spot(core, p)
-        return pltpu.make_async_copy(g.at[at], cg_hbm.at[at], out_sem.at[steps + p])
-
-    def gradient(p, _):
+        return pltpu.make_async_copy(g.at[at], cg_hbm.at[at], out_sem.at[len(flows) + p])
+
+    def gradient(p):
         for i, which in enumerate((1 - core, core)):
             for c in range(steps * RING):
                 scaled = factor[c, pl.ds(which * pieces + p, 1), :]
@@ -350,84 +360,104 @@
     def q_ready(s):
         pltpu.make_async_copy(q_hbm.at[s], q.at[s], in_sem.at[q_sem + s]).wait()
 
-    tables(0)
+    for s in range(steps):
+        tables(s)
     load_c.wait()
     for load in loads_f:
         load.wait()
-    for s in range(1, steps):
-        load_q(s)
     prepare(0, 1)
     q_ready(0)
     pl.semaphore_wait(barrier, len(peers))
 
     plan = [
-        ("s", 0, 0, []),
-        ("s", 0, 1, [(stat_send, 0, 0), (prepare, 1, steps), (tables, 1), (tables, 2), (q_ready, 1), (q_ready, 2)]),
-        ("s", 1, 0, [(stat_merge, 0, 0)]),
-        ("s", 1, 1, [(stat_send, 1, 0), (stat_merge, 0, 1)]),
-        ("t", 0, 0, [(push, 0, 0, 1)]),
-        ("s", 2, 0, [(stat_merge, 1, 0)]),
-        ("s", 2, 1, [(stat_send, 2, 0)]),
-        ("t", 0, 1, [(stat_merge, 2, 0), (push, 0, 2), (stat_merge, 1, 1)]),
-        ("t", 0, 2, [(push, 0, 4)]),
-        ("t", 0, 3, [(relay1, 0), (stat_merge, 2, 1)]),
-        ("g", 0, 0, []),
-        ("t", 1, 0, [(push, 1, 0, 1), (pair_add, 0)]),
-        ("t", 1, 1, [(push, 1, 2)]),
-        ("t", 1, 2, [(push, 1, 4)]),
-        ("g", 1, 0, [(finish1, 0)]),
-        ("t", 1, 3, [(relay1, 1), (pair_add, 1)]),
-        ("t", 2, 0, [(push, 2, 0, 1), (relay2, 0)]),
-        ("t", 2, 1, [(push, 2, 2)]),
-        ("g", 2, 0, []),
-        ("t", 2, 2, [(push, 2, 4), (finish2, 0), (pair_add, 2)]),
-        ("t", 2, 3, []),
-        ("g", 3, 0, [(finish1, 1)]),
+        ("s", []),
+        ("s", [(stat_send, 0, 0), (prepare, 1, steps), (q_ready, 1), (q_ready, 2)]),
+        ("s", [(stat_merge, 0, 0)]),
+        ("s", [(stat_send, 1, 0), (stat_merge, 0, 1)]),
+        ("t", [(push, 0, 0, 1)]),
+        ("s", [(stat_merge, 1, 0)]),
+        ("t", [(push, 0, 2)]),
+        ("t", [(push, 0, 4)]),
+        ("s", [(stat_send, 2, 0), (stat_merge, 1, 1), (relay1, 0)]),
+        ("t", []),
+        ("t", [(stat_merge, 2, 0), (push, 0, 6, 7), (push, 1, 0, 1)]),
+        ("t", [(push, 1, 2)]),
+        ("t", [(push, 1, 4), (stat_merge, 2, 1)]),
+        ("g", [(pair_add, 0)]),
+        ("t", [(finish1, 0)]),
+        ("t", [(relay1, 1), (push, 2, 0, 1)]),
+        ("g", [(pair_add, 1), (relay2, 0)]),
+        ("t", [(push, 2, 2)]),
+        ("t", [(push, 2, 4), (push, 3, 0, 1)]),
+        ("g", [(pair_add, 2), (finish2, 0)]),
+        ("t", [(finish1, 1)]),
+        ("g", [(relay1, 2), (push, 3, 2, 4), (pair_add, 3)]),
     ]
-
-    @pl.loop(0, len(plan))
-    def _(n):
-        for name, work in (("s", scores), ("t", terms), ("g", gradient)):
-            mine = [(i, entry) for i, entry in enumerate(plan) if entry[0] == name]
-
-            @pl.when(functools.reduce(jnp.logical_or, [n == i for i, _ in mine]))
-            def _(mine=mine, work=work):
-                work(sum(jnp.where(n == i, entry[1], 0) for i, entry in mine), sum(jnp.where(n == i, entry[2], 0) for i, entry in mine))
-
-        for i, entry in enumerate(plan):
-            if entry[3]:
-                @pl.when(n == i)
-                def _(todo=entry[3]):
-                    for call, *args in todo:
-                        call(*args)
-
-    pair_add(3)
+    group = 6
+
+    def unit(n, counts):
+        after = []
+        for (name, work), count in zip((("s", scores), ("t", terms), ("g", gradient)), counts):
+            bits = sum(1 << i for i, entry in enumerate(plan) if entry[0] == name)
+            mine = lax.rem(lax.shift_right_logical(jnp.int32(bits), n), 2)
+
+            @pl.when(mine == 1)
+            def _(work=work, count=count):
+                work(count)
+
+            after.append(count + mine)
+        for begin in range(0, len(plan), group):
+            @pl.when((n >= begin) & (n < begin + group))
+            def _(begin=begin):
+                for i, entry in enumerate(plan[begin:begin + group], begin):
+                    if entry[1]:
+                        @pl.when(n == i)
+                        def _(todo=entry[1]):
+                            for call, *args in todo:
+                                call(*args)
+        return tuple(after)
+
+    lax.fori_loop(0, len(plan), unit, (jnp.int32(0),) * 3)
+
     far_add(0)
     relay2(1)
-    relay1(2)
+    relay1(3)
     far_add(1)
     finish2(1)
+    finish1(2)
+    finish1(3)
+    relay2(2)
+    relay2(3)
+    finish2(2)
     finish3(0)
     far_add(2)
-    finish1(2)
-    relay2(2)
+    finish2(3)
+    far_add(3)
     finish3(1)
-    finish2(2)
-    far_add(3)
-    finish3(2)
     for s in range(steps):
         for stage in range(2):
             for copy in stat_copy(s, stage):
                 copy.wait_send()
-        for i in range(6):
-            ring1(s, i).wait_send()
-            ring2(s, i).wait_send()
-        last(s).wait_send()
-        out_copy(s).wait()
+    for f in range(len(flows)):
+        for i in range(6 if f else 8):
+            ring1(f, i).wait_send()
     for p in range(pieces):
         pair_copy(p).wait_send()
+    finish3(2)
+    for f in range(steps - 1):
+        for i in range(6):
+            ring2(f, i).wait_send()
+        last(f).wait_send()
+        out_copy(f).wait()
+    for p in range(pieces):
         final_local(p).wait()
         final_copy(p).wait()
+    finish3(3)
+    for f in range(steps - 1, len(flows)):
+        for i in range(6):
+            ring2(f, i).wait_send()
+        last(f).wait_send()
+        out_copy(f).wait()
 
 
 def publish(a_ref, b_ref, a_out, b_out, a_buf, b_buf, sems):
@@ -463,13 +493,15 @@
     blocks = cols // BLK
     half, part = rows // 2, rows // RING // 2
     pieces = cols // 2 // BLK
-    messages = steps * 23 + 3 * pieces
+    split = width // 3 * 2
+    flows = steps + 1
+    messages = steps * 10 + flows * 13 + 3 * pieces + 2
     vmem = pl.BlockSpec(memory_space=pltpu.VMEM)
     smem = pl.BlockSpec(memory_space=pltpu.SMEM)
     anywhere = pl.BlockSpec(memory_space=pl.ANY)
     small = pltpu.VMEM((chunks, blocks, rows), F32)
     a, b = pl.pallas_call(
-        kernel,
+        functools.partial(kernel, split),
         out_shape=(
             jax.ShapeDtypeStruct((steps, share, width), F32),
             jax.ShapeDtypeStruct((cols, width), F32),
@@ -500,7 +532,7 @@
             pltpu.VMEM((pieces, BLK, width), F32),
             pltpu.VMEM((pieces, BLK, width), F32),
             pltpu.SemaphoreType.DMA((1 + fresh.shape[0] // rows + steps,)),
-            pltpu.SemaphoreType.DMA((steps + pieces,)),
+            pltpu.SemaphoreType.DMA((flows + pieces,)),
             pltpu.SemaphoreType.DMA((messages,)),
             pltpu.SemaphoreType.DMA((messages,)),
         ],

time: 91.3 us -> 89.3 us (0.978); the launches traced: 91.2 us -> 87.8 us
  Pallas kernels: 90.5 us -> 87.2 us
    pallas_call x1, Pallas kernels: 87.6 us -> 84.3 us  [on_device(): pl.pallas_call(functools.partial(kernel, split), out_shape=(jax.ShapeDtyp...]
where the time goes in v4:
time: 89.3 us; the launch traced here: 87.8 us
  Pallas kernels  87.2 us (98%)
    pallas_call x1, Pallas kernels, on_device(): pl.pallas_call(functools.partial(kernel, split), out_shape=(jax.ShapeDtyp...  84.3 us
    pallas_call x1, Pallas kernels, on_device(): pl.pallas_call(publish, out_shape=(jax.ShapeDtypeStruct(a.shape, F32), ja...  2.9 us

profile of v4, /device:TPU:0, one launch (start us, length us, event | category | flops | bytes accessed | tf_op | source)
XLA Modules:
  0.0 87.8 jit_solution(15322549737433922912)
XLA Ops:
  0.6 84.3 %cache_step.1 = (f32[3,32,768]{2,1,0:T(8,128)}, f32[1024,768]{1,0:T(8,128)}) custom-call(bf16[3,1024,768]{2,1,0:T(8,128)(2,1)} %q_hbm.1, s32[3,1024]{1,0:T(4,128)} %pos_ref.1, s32[3,8,192]{2,1,0:T(8,128)} %list_ref.1, s32[3,8]{1,0:T(4,128)} %count_ref.1, s32[3]{0:T(128)} %owner_ref.1, f32[1024,768]{1,0:T(8,128)} %cache_hbm.1, f32[512,768]{1,0:T(8,128)} %fresh_hbm.1), custom_call_target="tpu_custom_call" | custom-call | tf_op jit(solution)/shard_map/cache_step/pallas_call | solution.py:503
  84.9 2.9 %publish.1 = (f32[3,32,768]{2,1,0:T(8,128)}, f32[1024,768]{1,0:T(8,128)}) custom-call(f32[3,32,768]{2,1,0:T(8,128)} %get-tuple-element.4.a_ref, f32[1024,768]{1,0:T(8,128)} %get-tuple-element.5.b_ref), custom_call_target="tpu_custom_call" | custom-call | tf_op jit(solution)/shard_map/publish/pallas_call | solution.py:544

commit v5 on v4

--- a/solution.py
+++ b/solution.py
@@ -75,14 +75,22 @@
     across = [first(1), first(2), first(3)]
     peers = near + across + [far_peer, pair_peer]
 
-    def remote(number, src, dst, device):
+    def remote(out, into, src, dst, device):
         return pltpu.make_async_remote_copy(
-            src_ref=src, dst_ref=dst, send_sem=send_sem.at[number], recv_sem=recv_sem.at[number],
+            src_ref=src, dst_ref=dst, send_sem=send_sem.at[out], recv_sem=recv_sem.at[into],
             device_id=device, device_id_type=pl.DeviceIdType.MESH,
         )
 
-    stat_messages = len(near) + len(across)
-    base0 = steps * stat_messages
+    out1 = 2 * steps
+    out2, out3 = out1 + len(flows), out1 + 2 * len(flows)
+    out_pair = out1 + 3 * len(flows)
+    in1 = 2 * steps
+    in2, in3 = in1 + 3 * len(flows), in1 + 6 * len(flows)
+    in_pair = in1 + 7 * len(flows)
+
+    def whole(out, into, ref):
+        return remote(out, into, ref, ref, z_peer)
+
     barrier = pltpu.get_barrier_semaphore()
     for peer in peers:
         pl.semaphore_signal(barrier, inc=1, device_id=peer, device_id_type=pl.DeviceIdType.MESH)
@@ -192,21 +200,23 @@
             stat_out[s, 0, pl.ds(RING + a, 1), :] = total
 
     def stat_copy(s, stage):
-        base = s * stat_messages + stage * len(near)
+        number = 2 * s + stage
         return [
-            remote(base + i, stat_out.at[s, stage], stat_in.at[s, stage, i], device)
+            remote(number, number, stat_out.at[s, stage], stat_in.at[s, stage, i], device)
             for i, device in enumerate(across if stage else near)
         ]
+
+    def stat_all(s, stage):
+        number = 2 * s + stage
+        return whole(number, number, stat_in.at[s, stage, pl.ds(0, len(across) if stage else len(near))])
 
     def stat_send(s, stage):
         for copy in stat_copy(s, stage):
             copy.start()
 
     def stat_merge(s, stage):
-        copies = stat_copy(s, stage)
-        for copy in copies:
-            copy.wait_recv()
-        got = [stat_out[s, stage]] + [stat_in[s, stage, i] for i in range(len(copies))]
+        stat_all(s, stage).wait_recv()
+        got = [stat_out[s, stage]] + [stat_in[s, stage, i] for i in range(len(across) if stage else len(near))]
         tops = [v[:RING] for v in got]
         top = functools.reduce(jnp.maximum, tops)
         total = sum(v[RING:] * jnp.exp(p - top) for v, p in zip(got, tops))
@@ -225,15 +235,23 @@
 
     def ring1(f, i):
         s, along = flows[f]
-        number = base0 + f * 13 + i
+        into = in1 + 3 * f + min(i, 2)
         if f == 0 and i in (3, 5, 6, 7):
             along = pl.ds(0 if i < 6 else width // 2, width // 2)
             if i >= 6:
-                number, i = base0 + len(flows) * 13 + 3 * (cols // 2 // BLK) + i - 6, 2 * i - 9
+                i = 2 * i - 9
         right, left = first(1), first(3)
         low, high = pl.ds(0, half), pl.ds(half, half)
         k, side, device = [(0, low, right), (0, high, left), (1, high, right), (1, low, right), (2, low, left), (2, high, left)][i]
-        return remote(number, t.at[s, k, side, along], r1.at[s, i, :, along], device)
+        return remote(out1 + f, into, t.at[s, k, side, along], r1.at[s, i, :, along], device)
+
+    def arrived(f, into, ref):
+        s, along = flows[f]
+        whole(0, into + 3 * f + 2, ref.at[s, pl.ds(2, 4), :, along]).wait_recv()
+
+    def left(f, out, ref):
+        s, along = flows[f]
+        whole(out + f, 0, ref.at[s, :, :, along]).wait_send()
 
     def terms(count):
         s, k = count // RING, count % RING
@@ -273,12 +291,11 @@
         s, along = flows[f]
         right, left = second(1), second(3)
         d, side, device = [(2, 0, right), (2, 1, left), (1, 1, right), (1, 0, right), (3, 0, left), (3, 1, left)][i]
-        return remote(base0 + f * 13 + 6 + i, piece(f, d, side), r2.at[s, i, :, along], device)
+        return remote(out2 + f, in2 + 3 * f + min(i, 2), piece(f, d, side), r2.at[s, i, :, along], device)
 
     def finish1(f):
         s, along = flows[f]
-        for i in (2, 3, 4, 5) if f else (2, 3, 4, 5, 6, 7):
-            ring1(f, i).wait_recv()
+        arrived(f, in1, r1)
         u[s, :half, along] = t[s, 3, :half, along] + r1[s, 3, :, along] + r1[s, 4, :, along]
         u[s, half:, along] = t[s, 3, half:, along] + r1[s, 2, :, along] + r1[s, 5, :, along]
         for i in (0, 1, 2, 4):
@@ -293,12 +310,11 @@
 
     def last(f):
         s, along = flows[f]
-        return remote(base0 + f * 13 + 12, piece(f, 0, 1 - zl), r3.at[s, :, along], z_peer)
+        return remote(out3 + f, in3 + f, piece(f, 0, 1 - zl), r3.at[s, :, along], z_peer)
 
     def finish2(f):
         s, along = flows[f]
-        for i in (2, 3, 4, 5):
-            ring2(f, i).wait_recv()
+        arrived(f, in2, r2)
         add(piece(f, 0, 0), r2.at[s, 3, :, along], r2.at[s, 4, :, along])
         add(piece(f, 0, 1), r2.at[s, 2, :, along], r2.at[s, 5, :, along])
         last(f).start()
@@ -315,24 +331,23 @@
 
     side = cols // 2
     pieces = side // BLK
-    base = base0 + len(flows) * 13
 
     def spot(which, p):
         return pl.ds(pl.multiple_of(which * side + p * BLK, BLK), BLK)
 
     def pair_copy(p):
-        return remote(base + p, g.at[spot(1 - core, p)], pair_in.at[p], pair_peer)
+        return remote(out_pair, in_pair + p, g.at[spot(1 - core, p)], pair_in.at[p], pair_peer)
 
     def far_copy(p):
-        return remote(base + pieces + p, g.at[spot(core, p)], far_in.at[p], far_peer)
+        return remote(out_pair + 2 + p, in_pair + pieces + p, g.at[spot(core, p)], far_in.at[p], far_peer)
 
     def final_copy(p):
         at = spot(core, p)
-        return remote(base + 2 * pieces + p, g.at[at], cg_hbm.at[at], pair_peer)
+        return remote(out_pair + 1, in_pair + 2 * pieces, g.at[at], cg_hbm.at[at], pair_peer)
 
     def final_local(p):
         at = spot(core, p)
-        return pltpu.make_async_copy(g.at[at], cg_hbm.at[at], out_sem.at[len(flows) + p])
+        return pltpu.make_async_copy(g.at[at], cg_hbm.at[at], out_sem.at[len(flows)])
 
     def gradient(p):
         for i, which in enumerate((1 - core, core)):
@@ -376,14 +391,14 @@
         ("s", [(stat_send, 1, 0), (stat_merge, 0, 1)]),
         ("t", [(push, 0, 0, 1)]),
         ("s", [(stat_merge, 1, 0)]),
+        ("s", [(stat_send, 2, 0)]),
         ("t", [(push, 0, 2)]),
-        ("t", [(push, 0, 4)]),
-        ("s", [(stat_send, 2, 0), (stat_merge, 1, 1), (relay1, 0)]),
-        ("t", []),
-        ("t", [(stat_merge, 2, 0), (push, 0, 6, 7), (push, 1, 0, 1)]),
-        ("t", [(push, 1, 2)]),
-        ("t", [(push, 1, 4), (stat_merge, 2, 1)]),
+        ("t", [(push, 0, 4), (stat_merge, 2, 0), (relay1, 0), (push, 0, 6, 7)]),
+        ("t", [(stat_merge, 1, 1)]),
+        ("t", [(push, 1, 0, 1)]),
+        ("t", [(push, 1, 2), (stat_merge, 2, 1)]),
         ("g", [(pair_add, 0)]),
+        ("t", [(push, 1, 4)]),
         ("t", [(finish1, 0)]),
         ("t", [(relay1, 1), (push, 2, 0, 1)]),
         ("g", [(pair_add, 1), (relay2, 0)]),
@@ -436,26 +451,22 @@
     finish3(1)
     for s in range(steps):
         for stage in range(2):
-            for copy in stat_copy(s, stage):
-                copy.wait_send()
+            stat_all(s, stage).wait_send()
     for f in range(len(flows)):
-        for i in range(6 if f else 8):
-            ring1(f, i).wait_send()
-    for p in range(pieces):
-        pair_copy(p).wait_send()
+        left(f, out1, r1)
+    whole(out_pair, 0, pair_in).wait_send()
     finish3(2)
     for f in range(steps - 1):
-        for i in range(6):
-            ring2(f, i).wait_send()
+        left(f, out2, r2)
         last(f).wait_send()
         out_copy(f).wait()
-    for p in range(pieces):
-        final_local(p).wait()
-        final_copy(p).wait()
+    mine = pl.ds(pl.multiple_of(core * side, side), side)
+    rest = pl.ds(pl.multiple_of((1 - core) * side, side), side)
+    pltpu.make_async_copy(g.at[mine], cg_hbm.at[mine], out_sem.at[len(flows)]).wait()
+    remote(out_pair + 1, in_pair + 2 * pieces, g.at[mine], cg_hbm.at[rest], pair_peer).wait()
     finish3(3)
     for f in range(steps - 1, len(flows)):
-        for i in range(6):
-            ring2(f, i).wait_send()
+        left(f, out2, r2)
         last(f).wait_send()
         out_copy(f).wait()
 
@@ -495,7 +506,8 @@
     pieces = cols // 2 // BLK
     split = width // 3 * 2
     flows = steps + 1
-    messages = steps * 10 + flows * 13 + 3 * pieces + 2
+    sends = 2 * steps + 3 * flows + 2 + pieces
+    arrivals = 2 * steps + 7 * flows + 2 * pieces + 1
     vmem = pl.BlockSpec(memory_space=pltpu.VMEM)
     smem = pl.BlockSpec(memory_space=pltpu.SMEM)
     anywhere = pl.BlockSpec(memory_space=pl.ANY)
@@ -532,9 +544,9 @@
             pltpu.VMEM((pieces, BLK, width), F32),
             pltpu.VMEM((pieces, BLK, width), F32),
             pltpu.SemaphoreType.DMA((1 + fresh.shape[0] // rows + steps,)),
-            pltpu.SemaphoreType.DMA((flows + pieces,)),
-            pltpu.SemaphoreType.DMA((messages,)),
-            pltpu.SemaphoreType.DMA((messages,)),
+            pltpu.SemaphoreType.DMA((flows + 1,)),
+            pltpu.SemaphoreType.DMA((sends,)),
+            pltpu.SemaphoreType.DMA((arrivals,)),
         ],
         compiler_params=pltpu.CompilerParams(
             collective_id=0, has_side_effects=True, vmem_limit_bytes=67_043_328

time: 89.3 us -> 88.3 us (0.989)
  Pallas kernels: 87.2 us -> 86.1 us
    pallas_call x1, Pallas kernels: 84.3 us -> 83.2 us  [on_device(): pl.pallas_call(functools.partial(kernel, split), out_shape=(jax.ShapeDtyp...]
where the time goes in v5:
time: 88.3 us; the launch traced here: 86.8 us
  Pallas kernels  86.1 us (98%)
    pallas_call x1, Pallas kernels, on_device(): pl.pallas_call(functools.partial(kernel, split), out_shape=(jax.ShapeDtyp...  83.2 us
    pallas_call x1, Pallas kernels, on_device(): pl.pallas_call(publish, out_shape=(jax.ShapeDtypeStruct(a.shape, F32), ja...  2.9 us

profile of v5, /device:TPU:0, one launch (start us, length us, event | category | flops | bytes accessed | tf_op | source)
XLA Modules:
  0.0 86.8 jit_solution(4615987813457071043)
XLA Ops:
  0.6 83.2 %cache_step.1 = (f32[3,32,768]{2,1,0:T(8,128)}, f32[1024,768]{1,0:T(8,128)}) custom-call(bf16[3,1024,768]{2,1,0:T(8,128)(2,1)} %q_hbm.1, s32[3,1024]{1,0:T(4,128)} %pos_ref.1, s32[3,8,192]{2,1,0:T(8,128)} %list_ref.1, s32[3,8]{1,0:T(4,128)} %count_ref.1, s32[3]{0:T(128)} %owner_ref.1, f32[1024,768]{1,0:T(8,128)} %cache_hbm.1, f32[512,768]{1,0:T(8,128)} %fresh_hbm.1), custom_call_target="tpu_custom_call" | custom-call | tf_op jit(solution)/shard_map/cache_step/pallas_call | solution.py:515
  83.9 2.9 %publish.1 = (f32[3,32,768]{2,1,0:T(8,128)}, f32[1024,768]{1,0:T(8,128)}) custom-call(f32[3,32,768]{2,1,0:T(8,128)} %get-tuple-element.4.a_ref, f32[1024,768]{1,0:T(8,128)} %get-tuple-element.5.b_ref), custom_call_target="tpu_custom_call" | custom-call | tf_op jit(solution)/shard_map/publish/pallas_call | solution.py:556
